TPU v7x, 32 devices: a whole 2x2x4 slice. The times are simulated.
32 devices in a mesh: dp: 2 (over core), row: 4 (over y, x), col: 4 (over z).
Axes of the slice: x: 2, y: 2, z: 4, core: 2. Of those that a mesh axis runs over, the one named last changes fastest.
Arguments:
- block_input: bfloat16 [2048, 1024], P(('dp', 'row', 'col')), may hold values from -6 to 6
- seq_lengths: int32 [2, 5], P('dp'), may hold values from 1 to 512, 1024 in all within a row
- out_grad: bfloat16 [2048, 1024], P(('dp', 'row', 'col')), may hold values from -6 to 6
- attn_norm: float32 [1024], replicated, may hold values from 0.5 to 1.5
- query_weight: bfloat16 [1024, 1024], P('col', 'row'), may hold values from -0.1875 to 0.1875
- key_weight: bfloat16 [1024, 512], P('col', 'row'), may hold values from -0.1875 to 0.1875
- value_weight: bfloat16 [1024, 512], P('col', 'row'), may hold values from -0.1875 to 0.1875
- query_norm: float32 [64], replicated, may hold values from 0.5 to 1.5
- key_norm: float32 [64], replicated, may hold values from 0.5 to 1.5
- out_weight: bfloat16 [1024, 1024], P(('row', 'col')), may hold values from -0.75 to 0.75
- ffn_norm: float32 [1024], replicated, may hold values from 0.5 to 1.5
- gate_weight: bfloat16 [1024, 4608], P('col', 'row'), may hold values from -0.1875 to 0.1875
- up_weight: bfloat16 [1024, 4608], P('col', 'row'), may hold values from -0.1875 to 0.1875
- down_weight: bfloat16 [4608, 1024], P(('row', 'col')), may hold values from -0.09375 to 0.09375
Outputs:
- block_output: bfloat16 [2048, 1024], P(('dp', 'row', 'col'))
- input_grad: float32 [2048, 1024], P(('dp', 'row', 'col'))
- grad_attnnorm: float32 [1024], replicated
- grad_query: float32 [1024, 1024], P('col', 'row')
- grad_key: float32 [1024, 512], P('col', 'row')
- grad_value: float32 [1024, 512], P('col', 'row')
- grad_qnorm: float32 [64], replicated
- grad_knorm: float32 [64], replicated
- grad_outweight: float32 [1024, 1024], P(('row', 'col'))
- grad_ffnnorm: float32 [1024], replicated
- grad_gate: float32 [1024, 4608], P('col', 'row')
- grad_up: float32 [1024, 4608], P('col', 'row')
- grad_down: float32 [4608, 1024], P(('row', 'col'))
Inputs may be any that keep to these rules, and one draw needn't show every extreme that they name: Each row of seq_lengths sums to 1024, and its largest entry is exactly 512.
All inputs are finite; a program needn't handle non-finite values.
Results may differ from a plain program's by a relative error of at most 0.012.
The roundings to bfloat16 on the way count: a program that leaves them out, or rounds other values in their place, can miss the bound.
Values may be sent and summed in bfloat16 or wider, within the bound.
A program may use at most 128 MiB of HBM per device.

v0:
```python
import math

import jax
import jax.numpy as jnp
from jax import lax
from jax.sharding import PartitionSpec as P

EPSILON = 1e-05
THETA = 1000000.0


def segment_info(seq_lengths, length):
    end_points = jnp.cumsum(seq_lengths)
    places = jnp.arange(length, dtype=jnp.int32)
    passed = (places[:, None] >= end_points[None, :]).astype(jnp.int32)
    segment = jnp.sum(passed, axis=1)
    begins = jnp.sum(passed * seq_lengths[None, :], axis=1)
    return (segment, places - begins)


def rope_tables(position, width):
    half_width = width // 2
    exponent = jnp.arange(half_width, dtype=jnp.float32) * (2.0 / width)
    frequency = jnp.exp(-math.log(THETA) * exponent)
    angles = position.astype(jnp.float32)[:, None] * frequency[None, :]
    return (jnp.cos(angles), jnp.sin(angles))


def rotate(values, cosine, sine):
    half_width = values.shape[-1] // 2
    first_half = values[:, :half_width]
    second_half = values[:, half_width:]
    return jnp.concatenate(
        [first_half * cosine - second_half * sine, second_half * cosine + first_half * sine], axis=1
    )


def rotate_back(cotangent, cosine, sine):
    half_width = cotangent.shape[-1] // 2
    first_half = cotangent[:, :half_width]
    second_half = cotangent[:, half_width:]
    return jnp.concatenate(
        [first_half * cosine + second_half * sine, second_half * cosine - first_half * sine], axis=1
    )


def head_norm(values, gain_vec):
    inv_rms = lax.rsqrt(jnp.mean(values * values, axis=-1, keepdims=True) + EPSILON)
    return (values * inv_rms * gain_vec, inv_rms)


def head_norm_back(cotangent, values, inv_rms, gain_vec):
    normed = values * inv_rms
    weighted = cotangent * gain_vec
    gain_grad = jnp.sum(cotangent * normed, axis=0)
    inner_mean = jnp.mean(weighted * normed, axis=-1, keepdims=True)
    return (inv_rms * (weighted - normed * inner_mean), gain_grad)


def attend(queries, key_rows, value_rows, segment):
    length = queries.shape[0]
    block_rows = min(512, length)
    places = jnp.arange(length, dtype=jnp.int32)
    score_scale = 1.0 / math.sqrt(queries.shape[1])

    def one_block(number):
        offset = number * block_rows
        query_block = lax.dynamic_slice_in_dim(queries, offset, block_rows, 0)
        row_segment = lax.dynamic_slice_in_dim(segment, offset, block_rows, 0)
        row_places = offset + jnp.arange(block_rows, dtype=jnp.int32)
        allowed = (row_segment[:, None] == segment[None, :]) & (
            places[None, :] <= row_places[:, None]
        )
        scores = jnp.dot(query_block, key_rows.T, preferred_element_type=jnp.float32) * score_scale
        exponent = jnp.where(allowed, jnp.exp(scores), 0.0)
        log_total = jnp.log(jnp.sum(exponent, axis=1))
        probability = jnp.where(allowed, jnp.exp(scores - log_total[:, None]), 0.0).astype(
            jnp.bfloat16
        )
        output = jnp.dot(probability, value_rows, preferred_element_type=jnp.float32)
        return (output, log_total)

    outputs, totals = lax.map(one_block, jnp.arange(length // block_rows, dtype=jnp.int32))
    return (outputs.reshape(length, -1), totals.reshape(length))


def attend_back(queries, key_rows, value_rows, segment, output_rows, out_grads, log_total):
    length = queries.shape[0]
    block_rows = min(512, length)
    places = jnp.arange(length, dtype=jnp.int32)
    score_scale = 1.0 / math.sqrt(queries.shape[1])

    def one_block(carried, number):
        key_total, value_total = carried
        offset = number * block_rows
        query_block = lax.dynamic_slice_in_dim(queries, offset, block_rows, 0)
        row_segment = lax.dynamic_slice_in_dim(segment, offset, block_rows, 0)
        grad_block = lax.dynamic_slice_in_dim(out_grads, offset, block_rows, 0)
        out_block = lax.dynamic_slice_in_dim(output_rows, offset, block_rows, 0)
        total_block = lax.dynamic_slice_in_dim(log_total, offset, block_rows, 0)
        row_places = offset + jnp.arange(block_rows, dtype=jnp.int32)
        allowed = (row_segment[:, None] == segment[None, :]) & (
            places[None, :] <= row_places[:, None]
        )
        scores = jnp.dot(query_block, key_rows.T, preferred_element_type=jnp.float32) * score_scale
        probability = jnp.where(allowed, jnp.exp(scores - total_block[:, None]), 0.0).astype(
            jnp.bfloat16
        )
        value_total = value_total + jnp.dot(
            probability.T, grad_block, preferred_element_type=jnp.float32
        )
        prob_grad = jnp.dot(grad_block, value_rows.T, preferred_element_type=jnp.float32)
        row_delta = jnp.sum(
            grad_block.astype(jnp.float32) * out_block.astype(jnp.float32), axis=1, keepdims=True
        )
        score_grad = (
            score_scale * probability.astype(jnp.float32) * (prob_grad - row_delta)
        ).astype(jnp.bfloat16)
        query_grad = jnp.dot(score_grad, key_rows, preferred_element_type=jnp.float32)
        key_total = key_total + jnp.dot(
            score_grad.T, query_block, preferred_element_type=jnp.float32
        )
        return ((key_total, value_total), query_grad)

    zero_rows = jnp.zeros((length, queries.shape[1]), jnp.float32)
    (key_grad, value_grad), query_grads = lax.scan(
        one_block, (zero_rows, zero_rows), jnp.arange(length // block_rows, dtype=jnp.int32)
    )
    return (query_grads.reshape(length, -1), key_grad, value_grad)


def head_inputs(query_raw, key_raw, value_raw, query_norm, key_norm, cosine, sine):
    query_normed, query_scale = head_norm(query_raw, query_norm)
    key_normed, key_scale = head_norm(key_raw, key_norm)
    query_rot = rotate(query_normed, cosine, sine).astype(jnp.bfloat16)
    key_rot = rotate(key_normed, cosine, sine).astype(jnp.bfloat16)
    return (query_rot, key_rot, value_raw.astype(jnp.bfloat16), query_scale, key_scale)


def head_forward(query_raw, key_raw, value_raw, query_norm, key_norm, cosine, sine, segment):
    query_rot, key_rot, value_low, query_scale, key_scale = head_inputs(
        query_raw, key_raw, value_raw, query_norm, key_norm, cosine, sine
    )
    output, log_total = attend(query_rot, key_rot, value_low, segment)
    return (output.astype(jnp.bfloat16), log_total)


def head_backward(
    query_raw,
    key_raw,
    value_raw,
    query_norm,
    key_norm,
    cosine,
    sine,
    segment,
    attn_low,
    cat_grad,
    log_total,
):
    query_rot, key_rot, value_low, query_scale, key_scale = head_inputs(
        query_raw, key_raw, value_raw, query_norm, key_norm, cosine, sine
    )
    query_grad, key_grad, value_grad = attend_back(
        query_rot, key_rot, value_low, segment, attn_low, cat_grad, log_total
    )
    query_pre, query_gain = head_norm_back(
        rotate_back(query_grad, cosine, sine), query_raw, query_scale, query_norm
    )
    key_pre, key_gain = head_norm_back(
        rotate_back(key_grad, cosine, sine), key_raw, key_scale, key_norm
    )
    return (
        query_pre.astype(jnp.bfloat16),
        key_pre.astype(jnp.bfloat16),
        value_grad.astype(jnp.bfloat16),
        query_gain,
        key_gain,
    )


def gather_rows(values):
    return lax.all_gather(values, ("row", "col"), axis=0, tiled=True)


def project_rows(left_rows, right_matrix):
    return lax.psum_scatter(
        jnp.dot(left_rows, right_matrix, preferred_element_type=jnp.float32),
        ("row", "col"),
        scatter_dimension=0,
        tiled=True,
    )


def back_sum(partial_value, local_rows):
    row_count = lax.axis_size("row")
    col_count = lax.axis_size("col")
    shaped = partial_value.reshape(row_count, col_count, local_rows, partial_value.shape[1])
    summed = lax.psum_scatter(shaped, "row", scatter_dimension=0, tiled=True)
    swapped = lax.all_to_all(summed, "col", split_axis=1, concat_axis=3, tiled=True)
    return swapped.reshape(local_rows, -1)


def shards(
    block_input,
    seq_lengths,
    out_grad,
    attn_norm,
    query_weight,
    key_weight,
    value_weight,
    query_norm,
    key_norm,
    out_weight,
    ffn_norm,
    gate_weight,
    up_weight,
    down_weight,
):
    local_rows = block_input.shape[0]
    head_dim = query_norm.shape[0]
    col_width = query_weight.shape[0]
    col_index = lax.axis_index("col")
    slot_count = query_weight.shape[1] // head_dim
    residual = block_input.astype(jnp.float32)
    normed_in, scale_in = head_norm(residual, attn_norm)
    first_act = normed_in.astype(jnp.bfloat16)
    first_full = gather_rows(first_act)
    length = first_full.shape[0]
    first_cols = lax.dynamic_slice_in_dim(first_full, col_index * col_width, col_width, 1)
    segment, position = segment_info(seq_lengths[0], length)
    cosine, sine = rope_tables(position, head_dim)
    query_slots = query_weight.reshape(col_width, slot_count, head_dim)
    key_slots = jnp.repeat(key_weight.reshape(col_width, slot_count // 2, head_dim), 2, axis=1)
    value_slots = jnp.repeat(value_weight.reshape(col_width, slot_count // 2, head_dim), 2, axis=1)
    slot_weight = jnp.stack([query_slots, key_slots, value_slots], axis=2).reshape(
        col_width, slot_count * 3 * head_dim
    )
    partial_value = jnp.dot(first_cols, slot_weight, preferred_element_type=jnp.float32).reshape(
        length, slot_count, 3 * head_dim
    )
    own_sums = lax.psum_scatter(partial_value, "col", scatter_dimension=1, tiled=True)[:, 0, :]
    query_raw = own_sums[:, :head_dim]
    key_raw = own_sums[:, head_dim : 2 * head_dim]
    value_raw = own_sums[:, 2 * head_dim :]
    attn_low, log_total = head_forward(
        query_raw, key_raw, value_raw, query_norm, key_norm, cosine, sine, segment
    )
    middle = residual + project_rows(attn_low, out_weight)
    normed_mid, scale_mid = head_norm(middle, ffn_norm)
    second_act = normed_mid.astype(jnp.bfloat16)
    second_full = gather_rows(second_act)
    second_cols = lax.dynamic_slice_in_dim(second_full, col_index * col_width, col_width, 1)
    gate_part = jnp.dot(second_cols, gate_weight, preferred_element_type=jnp.float32)
    up_part = jnp.dot(second_cols, up_weight, preferred_element_type=jnp.float32)
    gating, upward = (
        lax.psum_scatter(gate_part, "col", scatter_dimension=1, tiled=True),
        lax.psum_scatter(up_part, "col", scatter_dimension=1, tiled=True),
    )
    sigmoid_gate = jax.nn.sigmoid(gating)
    activated = gating * sigmoid_gate
    hidden = (activated * upward).astype(jnp.bfloat16)
    result_sum = middle + project_rows(hidden, down_weight)
    block_output = result_sum.astype(jnp.bfloat16)
    out_full = gather_rows(out_grad)
    grad_down = jnp.dot(hidden.T, out_full, preferred_element_type=jnp.float32)
    hidden_grad = jnp.dot(out_full, down_weight.T, preferred_element_type=jnp.float32)
    gate_low = (hidden_grad * upward * sigmoid_gate * (1.0 + gating * (1.0 - sigmoid_gate))).astype(
        jnp.bfloat16
    )
    up_low = (hidden_grad * activated).astype(jnp.bfloat16)
    gate_full, up_full = (
        lax.all_gather(gate_low, "col", axis=1, tiled=True),
        lax.all_gather(up_low, "col", axis=1, tiled=True),
    )
    grad_gate = jnp.dot(second_cols.T, gate_full, preferred_element_type=jnp.float32)
    grad_up = jnp.dot(second_cols.T, up_full, preferred_element_type=jnp.float32)
    act_part = jnp.dot(gate_full, gate_weight.T, preferred_element_type=jnp.float32) + jnp.dot(
        up_full, up_weight.T, preferred_element_type=jnp.float32
    )
    act_grad2 = back_sum(act_part, local_rows)
    middle_back, ffn_gain_grad = head_norm_back(act_grad2, middle, scale_mid, ffn_norm)
    middle_grad = out_grad.astype(jnp.float32) + middle_back
    middle_full = gather_rows(middle_grad.astype(jnp.bfloat16))
    grad_outweight = jnp.dot(attn_low.T, middle_full, preferred_element_type=jnp.float32)
    cat_grad = jnp.dot(middle_full, out_weight.T, preferred_element_type=jnp.float32).astype(
        jnp.bfloat16
    )
    query_low, key_low, value_low, query_gain, key_gain = head_backward(
        query_raw,
        key_raw,
        value_raw,
        query_norm,
        key_norm,
        cosine,
        sine,
        segment,
        attn_low,
        cat_grad,
        log_total,
    )
    own_slot = jnp.concatenate([query_low, key_low, value_low], axis=1)[:, None, :]
    all_slots = lax.all_gather(own_slot, "col", axis=1, tiled=True).reshape(
        length, slot_count * 3 * head_dim
    )
    act_grad1 = back_sum(
        jnp.dot(all_slots, slot_weight.T, preferred_element_type=jnp.float32), local_rows
    )
    slot_grad = jnp.dot(first_cols.T, all_slots, preferred_element_type=jnp.float32).reshape(
        col_width, slot_count, 3, head_dim
    )
    grad_query = slot_grad[:, :, 0].reshape(col_width, slot_count * head_dim)
    grad_key = jnp.sum(
        slot_grad[:, :, 1].reshape(col_width, slot_count // 2, 2, head_dim), axis=2
    ).reshape(col_width, -1)
    grad_value = jnp.sum(
        slot_grad[:, :, 2].reshape(col_width, slot_count // 2, 2, head_dim), axis=2
    ).reshape(col_width, -1)
    input_back, attn_gain_grad = head_norm_back(act_grad1, residual, scale_in, attn_norm)
    input_grad = middle_grad + input_back
    grad_query, grad_key, grad_value, grad_outweight, grad_gate, grad_up, grad_down = lax.psum(
        (grad_query, grad_key, grad_value, grad_outweight, grad_gate, grad_up, grad_down), "dp"
    )
    grad_attnnorm, grad_qnorm, grad_knorm, grad_ffnnorm = lax.psum(
        (attn_gain_grad, query_gain, key_gain, ffn_gain_grad), ("dp", "row", "col")
    )
    return (
        block_output,
        input_grad,
        grad_attnnorm,
        grad_query,
        grad_key,
        grad_value,
        grad_qnorm,
        grad_knorm,
        grad_outweight,
        grad_ffnnorm,
        grad_gate,
        grad_up,
        grad_down,
    )


def solution(mesh):
    placed = (
        P(("dp", "row", "col"), None),
        P("dp", None),
        P(("dp", "row", "col"), None),
        P(),
        P("col", "row"),
        P("col", "row"),
        P("col", "row"),
        P(),
        P(),
        P(("row", "col"), None),
        P(),
        P("col", "row"),
        P("col", "row"),
        P(("row", "col"), None),
    )
    return jax.shard_map(
        shards,
        mesh=mesh,
        in_specs=placed,
        out_specs=(
            P(("dp", "row", "col"), None),
            P(("dp", "row", "col"), None),
            P(),
            P("col", "row"),
            P("col", "row"),
            P("col", "row"),
            P(),
            P(),
            P(("row", "col"), None),
            P(),
            P("col", "row"),
            P("col", "row"),
            P(("row", "col"), None),
        ),
        check_vma=False,
    )
```

profile of v0, /device:TPU:0, one launch (start us, length us, event | category | flops | bytes accessed | tf_op | source)
XLA Modules:
  0.0 1014.7 jit_solution(16867831467073007329)
XLA Ops:
  7.2 1.1 fusion.41
  8.9 1.7 fusion.35
  13.7 60.9 %all-gather.9.cloned.1.call-done = bf16[1024,1024]{1,0:T(8,128)(2,1)} async-done(((bf16[64,1024]{1,0:T(8,128)(2,1)}), bf16[1024,1024]{1,0:T(8,128)(2,1)}) %all-gather.9.cloned.1.call-update) | async-done | bytes 2097168 | tf_op jit(solution)/shard_map/all_gather | solution.py:183
  74.6 3.3 fusion.19
  78.8 58.5 %reduce-scatter.12.cloned.1.call-done = f32[1024,1,192]{0,2,1:T(8,128)} async-done(((f32[1024,4,192]{0,2,1:T(8,128)}), f32[1024,1,192]{0,2,1:T(8,128)}) %reduce-scatter.12.cloned.1.call-update) | async-done | bytes 786448 | tf_op jit(solution)/shard_map/reduce_scatter | solution.py:242
  137.3 1.1 multiply_reduce_fusion.8
  139.4 1.1 fusion.59
  142.4 8.1 while.28
  143.7 1.8 select_reduce_fusion.3
  147.8 1.8 select_reduce_fusion.3
  151.4 3.6 fusion.80
  155.0 97.4 %reduce-scatter.14.cloned.1.call-done = f32[64,1024]{1,0:T(8,128)} async-done(((f32[1024,1024]{1,0:T(8,128)}), f32[64,1024]{1,0:T(8,128)}) %reduce-scatter.14.cloned.1.call-update) | async-done | bytes 262160 | tf_op jit(solution)/shard_map/reduce_scatter | solution.py:187
  252.4 1.1 multiply_reduce_fusion.7
  255.0 59.7 %all-gather.11.cloned.1.call-done = bf16[1024,1024]{1,0:T(8,128)(2,1)} async-done(((bf16[64,1024]{1,0:T(8,128)(2,1)}), bf16[1024,1024]{1,0:T(8,128)(2,1)}) %all-gather.11.cloned.1.call-update) | async-done | bytes 2097168 | tf_op jit(solution)/shard_map/all_gather | solution.py:183
  314.6 4.0 fusion.31
  319.7 4.0 fusion.33
  323.8 52.7 %all-gather.13.cloned.1.call-done = bf16[1024,1024]{1,0:T(8,128)(2,1)} async-done(((bf16[64,1024]{1,0:T(8,128)(2,1)}), bf16[1024,1024]{1,0:T(8,128)(2,1)}) %all-gather.13.cloned.1.call-update) | async-done | bytes 2097168 | tf_op jit(solution)/shard_map/all_gather | solution.py:183
  376.6 86.3 %reduce-scatter.18.cloned.1.call-done = f32[1024,288]{0,1:T(8,128)} async-done(((f32[1024,1152]{0,1:T(8,128)}), f32[1024,288]{0,1:T(8,128)}) %reduce-scatter.18.cloned.1.call-update) | async-done | bytes 1179664 | tf_op jit(solution)/shard_map/reduce_scatter | solution.py:258
  462.9 88.1 %reduce-scatter.16.cloned.1.call-done = f32[1024,288]{0,1:T(8,128)} async-done(((f32[1024,1152]{0,1:T(8,128)}), f32[1024,288]{0,1:T(8,128)}) %reduce-scatter.16.cloned.1.call-update) | async-done | bytes 1179664 | tf_op jit(solution)/shard_map/reduce_scatter | solution.py:257
  551.0 4.7 multiply_convert_fusion.1
  556.5 49.9 %all-gather.15.cloned.1.call-done = bf16[1024,1152]{0,1:T(8,128)(2,1)} async-done(((bf16[1024,288]{0,1:T(8,128)(2,1)}), bf16[1024,1152]{0,1:T(8,128)(2,1)}) %all-gather.15.cloned.1.call-update) | async-done | bytes 2359312 | tf_op jit(solution)/shard_map/all_gather | solution.py:273
  606.3 2.7 fusion.82
  609.0 48.3 %all-gather.17.cloned.1.call-done = bf16[1024,1152]{0,1:T(8,128)(2,1)} async-done(((bf16[1024,288]{0,1:T(8,128)(2,1)}), bf16[1024,1152]{0,1:T(8,128)(2,1)}) %all-gather.17.cloned.1.call-update) | async-done | bytes 2359312 | tf_op jit(solution)/shard_map/all_gather | solution.py:274
  657.3 3.5 convolution_add_fusion.2
  660.9 26.8 %reduce-scatter.22.cloned.1.call-done = f32[1,4,64,256]{3,2,1,0:T(8,128)} async-done(((f32[4,4,64,256]{3,2,1,0:T(8,128)}), f32[1,4,64,256]{3,2,1,0:T(8,128)}) %reduce-scatter.22.cloned.1.call-update) | async-done | bytes 262160
  687.7 13.3 %all_to_all.30 = f32[1,4,64,256]{3,2,0,1:T(8,128)S(1)} all-to-all(f32[1,4,64,256]{3,2,0,1:T(8,128)} %bitcast.165), channel_id=1, replica_groups=mesh['dp'=2,'row'=4,'col'=4] {'col'}, dimensions={1} | all-to-all | bytes 524288 | tf_op jit(solution)/shard_map/all_to_all | solution.py:200
  703.7 57.9 %all-gather.19.cloned.1.call-done = bf16[1024,1024]{1,0:T(8,128)(2,1)} async-done(((bf16[64,1024]{1,0:T(8,128)(2,1)}), bf16[1024,1024]{1,0:T(8,128)(2,1)}) %all-gather.19.cloned.1.call-update) | async-done | bytes 2097168 | tf_op jit(solution)/shard_map/all_gather | solution.py:183
  761.6 3.0 convolution_convert_fusion
  765.1 27.0 %while.29 = (s32[]{:T(128)}, f32[1024,64]{0,1:T(8,128)}, f32[1024,64]{0,1:T(8,128)S(1)}, f32[2,512,64]{1,0,2:T(2,128)}, s32[2]{0:T(128)}, /*index=5*/s32[1024]{0...) while((s32[]{:T(128)}, f32[1024,64]{0,1:T(8,128)}, ...), condition=%wide.region_19.20_spmd.clone, body=%wide.region_17.19_spmd.clone.sunk | while | flops 342228992 | bytes 10248498 | solution.py:126
  765.1 1.2 dynamic_slice.88
  767.8 1.7 select_convert_fusion.6
  770.5 1.1 multiply_reduce_fusion.11
  772.7 3.5 dynamic_update_slice.20
  776.2 2.0 convolution_add_fusion.5
  778.5 1.3 dynamic_slice.88
  781.3 1.7 select_convert_fusion.6
  784.0 1.1 multiply_reduce_fusion.11
  786.2 3.5 dynamic_update_slice.20
  789.7 2.1 convolution_add_fusion.5
  792.1 1.1 copy.128
  793.2 1.6 fusion.68
  794.8 1.8 multiply_reduce_fusion.2
  797.7 35.9 %all-gather.21.cloned.1.call-done = bf16[1024,768]{0,1:T(8,128)(2,1)} async-done(((bf16[1024,192]{0,1:T(8,128)(2,1)}), bf16[1024,768]{0,1:T(8,128)(2,1)}) %all-gather.21.cloned.1.call-update) | async-done | bytes 1572880 | tf_op jit(solution)/shard_map/all_gather | solution.py:303
  833.6 1.7 copy.99
  835.3 1.6 fusion.83
  837.0 3.2 fusion.81
  840.3 3.5 fusion.85
  843.8 1.9 fusion.27
  845.8 1.9 fusion.29
  847.7 2.3 fusion.84
  850.0 1.6 fusion.17
  853.9 9.9 reduce-scatter.24.cloned.1.call-done
  863.9 18.3 %all_to_all.31 = f32[1,4,64,256]{3,2,0,1:T(8,128)S(1)} all-to-all(f32[1,4,64,256]{3,2,0,1:T(8,128)} %bitcast.163), channel_id=1, replica_groups=mesh['dp'=2,'row'=4,'col'=4] {'col'}, dimensions={1} | all-to-all | bytes 524288 | tf_op jit(solution)/shard_map/all_to_all | solution.py:200
  882.7 41.9 %all-reduce.2 = (f32[1024]{0:T(1024)}, f32[64]{0:T(128)}, f32[64]{0:T(128)}, f32[1024]{0:T(1024)}) all-reduce(f32[1024]{0:T(1024)S(1)} %get-tuple-element.323, f32[64]{0:T(128)S(1)} %copy-done.39, f32[64]{0:T(128)S(1)} %get-tuple-element.313, f32[1024]{0:T(1024)S(1)} %copy-done.28), channel_id=1, replica_groups=mesh['dp'=2,'row'=4,'col'=4] {'dp','row','col'}, use_global_device_ids=true, to_apply=%region_25.26 | all-reduce | flops 2176 | bytes 17408 | tf_op jit(solution)/shard_map/psum | solution.py:324
  924.6 39.8 %reduce-scatter.20.cloned.1.call-done = f32[64,1024]{1,0:T(8,128)} async-done(((f32[1024,1024]{1,0:T(8,128)}), f32[64,1024]{1,0:T(8,128)}) %reduce-scatter.20.cloned.1.call-update) | async-done | bytes 262160 | tf_op jit(solution)/shard_map/reduce_scatter | solution.py:187
  964.4 1.9 fusion.39
  966.3 30.7 %all-reduce.6.cloned.1.call-done = (f32[256,256]{1,0:T(8,128)}, f32[256,128]{0,1:T(8,128)}, f32[256,128]{0,1:T(8,128)}, f32[64,1024]{1,0:T(8,128)}, f32[256,1152...) async-done(((f32[256,256]{1,0:T(8,128)}, f32[256,128]{0,1:T(8,128)}, f32[256,128]{0,1:T(8,128)}, f32[64,1024]{1,0:T(8,128)}, f32[256,1152]{1,0:T(8,128)}, ...) | async-done | bytes 4325392 | tf_op jit(solution)/shard_map/psum | solution.py:321
  997.0 1.8 copy.104
  998.7 1.7 copy.105
  1000.4 1.7 copy.165
  1002.0 1.7 copy.166
  1003.7 2.5 copy.167
  1006.2 1.0 copy.168
  1007.2 1.0 copy.169
  (197 shorter events, 28.2 us)
Async XLA Ops:
  7.2 543.8 %copy-start = (bf16[288,1024]{1,0:T(8,128)(2,1)S(1)}, bf16[288,1024]{1,0:T(8,128)(2,1)}, u32[]{:S(2)}) copy-start(bf16[288,1024]{1,0:T(8,128)(2,1)} %param.31) | copy-start | bytes 1769476
  7.2 67.4 %all-gather.9.cloned.1.call-start = ((), (), s32[]{:S(2)}) async-start(), calls=%async_computation.9 | async-start | bytes 2228224 | tf_op jit(solution)/shard_map/all_gather | solution.py:183
  8.3 0.6 copy-start.35
  10.6 126.7 %reduce-scatter.12.cloned.1.call-start = ((), (), s32[]{:S(2)}) async-start(), calls=%async_computation.10 | async-start | bytes 3932160 | tf_op jit(solution)/shard_map/reduce_scatter | solution.py:242
  13.7 64.2 %copy-start.10 = (bf16[256,4,3,64]{0,3,2,1:T(8,128)(2,1)}, bf16[256,4,3,64]{0,3,2,1:T(8,128)(2,1)S(1)}, u32[]{:S(2)}) copy-start(bf16[256,4,3,64]{0,3,2,1:T(8,128)(2,1)S(1)} %copy.87) | copy-start | bytes 1179652
  77.9 0.7 copy-start.41
  77.9 61.5 %copy-start.31 = (f32[64]{0:T(128)S(1)}, f32[64]{0:T(128)}, u32[]{:S(2)}) copy-start(f32[64]{0:T(128)} %param.26) | copy-start | bytes 772
  77.9 61.5 %copy-start.33 = (f32[64]{0:T(128)S(1)}, f32[64]{0:T(128)}, u32[]{:S(2)}) copy-start(f32[64]{0:T(128)} %param.25) | copy-start | bytes 772
  77.9 174.5 %reduce-scatter.14.cloned.1.call-start = ((), (), s32[]{:S(2)}) async-start(), calls=%async_computation.11 | async-start | bytes 4456448 | tf_op jit(solution)/shard_map/reduce_scatter | solution.py:187
  78.7 63.6 %copy-start.40 = (f32[32]{0:T(128)}, f32[32]{0:T(128)S(1)}, u32[]{:S(2)}) copy-start(f32[32]{0:T(128)S(1)} %multiply_exponential_fusion) | copy-start | bytes 388
  78.8 63.5 %copy-start.27 = (f32[1024]{0:T(1024)}, f32[1024]{0:T(1024)S(1)}, u32[]{:S(2)}) copy-start(f32[1024]{0:T(1024)S(1)} %subtract_convert_fusion) | copy-start | bytes 12292
  142.4 9.0 copy-start.24
  154.9 97.5 %copy-start.12 = (bf16[64,1024]{1,0:T(8,128)(2,1)S(1)}, bf16[64,1024]{1,0:T(8,128)(2,1)}, u32[]{:S(2)}) copy-start(bf16[64,1024]{1,0:T(8,128)(2,1)} %param.18) | copy-start | bytes 393220
  154.9 98.6 %copy-start.25 = (f32[1024]{0:T(1024)S(1)}, f32[1024]{0:T(1024)}, u32[]{:S(2)}) copy-start(f32[1024]{0:T(1024)} %param.28) | copy-start | bytes 12292
  154.9 159.7 %copy-start.14 = (bf16[256,1152]{1,0:T(8,128)(2,1)S(1)}, bf16[256,1152]{1,0:T(8,128)(2,1)}, u32[]{:S(2)}) copy-start(bf16[256,1152]{1,0:T(8,128)(2,1)} %param.30) | copy-start | bytes 1769476
  155.0 159.7 %all-gather.11.cloned.1.call-start = ((), (), s32[]{:S(2)}) async-start(), calls=%async_computation.12 | async-start | bytes 2228224 | tf_op jit(solution)/shard_map/all_gather | solution.py:183
  253.5 448.5 %copy-start.5 = (f32[64,1024]{1,0:T(8,128)}, f32[64,1024]{1,0:T(8,128)S(1)}, u32[]{:S(2)}) copy-start(f32[64,1024]{1,0:T(8,128)S(1)} %get-tuple-element.379) | copy-start | bytes 786436
  253.5 448.4 %copy-start.29 = (f32[64]{0:T(128)}, f32[64]{0:T(128)S(1)}, u32[]{:S(2)}) copy-start(f32[64]{0:T(128)S(1)} %add_rsqrt_fusion.2) | copy-start | bytes 772
  254.3 122.3 %all-gather.13.cloned.1.call-start = ((), (), s32[]{:S(2)}) async-start(), calls=%async_computation.16 | async-start | bytes 2228224 | tf_op jit(solution)/shard_map/all_gather | solution.py:183
  254.9 207.9 %reduce-scatter.18.cloned.1.call-start = ((), (), s32[]{:S(2)}) async-start(), calls=%async_computation.14 | async-start | bytes 5898240 | tf_op jit(solution)/shard_map/reduce_scatter | solution.py:258
  318.7 1.1 copy-start.23
  318.7 232.3 %reduce-scatter.16.cloned.1.call-start = ((), (), s32[]{:S(2)}) async-start(), calls=%async_computation.13 | async-start | bytes 5898240 | tf_op jit(solution)/shard_map/reduce_scatter | solution.py:257
  323.8 282.5 %all-gather.15.cloned.1.call-start = ((), (), s32[]{:S(2)}) async-start(), calls=%async_computation.17 | async-start | bytes 2949120 | tf_op jit(solution)/shard_map/all_gather | solution.py:273
  555.7 101.6 %all-gather.17.cloned.1.call-start = ((), (), s32[]{:S(2)}) async-start(), calls=%async_computation.18 | async-start | bytes 2949120 | tf_op jit(solution)/shard_map/all_gather | solution.py:274
  556.4 131.3 %reduce-scatter.22.cloned.1.call-start = ((), (), s32[]{:S(2)}) async-start(), calls=%async_computation.21 | async-start | bytes 1310720
  660.8 41.2 %copy-start.21 = (bf16[64,1024]{1,0:T(8,128)(2,1)S(1)}, bf16[64,1024]{1,0:T(8,128)(2,1)}, u32[]{:S(2)}) copy-start(bf16[64,1024]{1,0:T(8,128)(2,1)} %param.20) | copy-start | bytes 393220
  660.8 100.7 %all-gather.19.cloned.1.call-start = ((), (), s32[]{:S(2)}) async-start(), calls=%async_computation.19 | async-start | bytes 2228224 | tf_op jit(solution)/shard_map/all_gather | solution.py:183
  701.2 0.7 copy-start.8
  702.0 63.1 %copy-start.37 = (f32[64]{0:T(128)}, f32[64]{0:T(128)S(1)}, u32[]{:S(2)}) copy-start(f32[64]{0:T(128)S(1)} %broadcast_multiply_fusion.3) | copy-start | bytes 772
  702.8 130.8 %all-gather.21.cloned.1.call-start = ((), (), s32[]{:S(2)}) async-start(), calls=%async_computation.20 | async-start | bytes 1966080 | tf_op jit(solution)/shard_map/all_gather | solution.py:303
  765.1 6.5 copy-start.2
  776.2 2.3 copy-start.3
  778.5 6.6 copy-start.2
  789.7 2.4 copy-start.3
  792.1 4.5 copy-start.7
  792.1 4.5 copy-start.32
  792.1 4.5 copy-start.34
  796.8 38.5 %copy-start.11 = (bf16[256,4,3,64]{0,3,2,1:T(8,128)(2,1)S(1)}, bf16[256,4,3,64]{0,3,2,1:T(8,128)(2,1)}, u32[]{:S(2)}) copy-start(bf16[256,4,3,64]{0,3,2,1:T(8,128)(2,1)} %copy-done.10) | copy-start | bytes 1179652
  797.6 66.3 %reduce-scatter.24.cloned.1.call-start = ((), (), s32[]{:S(2)}) async-start(), calls=%async_computation.22 | async-start | bytes 1310720
  835.3 1.7 copy-start.17
  836.9 127.5 %reduce-scatter.20.cloned.1.call-start = ((), (), s32[]{:S(2)}) async-start(), calls=%async_computation.15 | async-start | bytes 4456448 | tf_op jit(solution)/shard_map/reduce_scatter | solution.py:187
  840.2 3.6 copy-start.1
  840.2 156.7 %all-reduce.6.cloned.1.call-start = ((), (), s32[]{:S(2)}) async-start(), calls=%async_computation.23 | async-start | bytes 8650752 | tf_op jit(solution)/shard_map/psum | solution.py:321
  840.3 3.5 copy-start.16
  843.8 1.9 copy-start.15
  845.7 1.9 copy-start.4
  847.7 2.3 copy-start.18
  853.8 28.6 %copy-start.13 = (bf16[64,1024]{1,0:T(8,128)(2,1)S(1)}, bf16[64,1024]{1,0:T(8,128)(2,1)}, u32[]{:S(2)}) copy-start(bf16[64,1024]{1,0:T(8,128)(2,1)} %param.18) | copy-start | bytes 393220
  853.8 28.6 %copy-start.26 = (f32[1024]{0:T(1024)S(1)}, f32[1024]{0:T(1024)}, u32[]{:S(2)}) copy-start(f32[1024]{0:T(1024)} %param.21) | copy-start | bytes 12292
  853.9 28.6 %copy-start.36 = (f32[64]{0:T(128)S(1)}, f32[64]{0:T(128)}, u32[]{:S(2)}) copy-start(f32[64]{0:T(128)} %copy-done.35) | copy-start | bytes 772
  853.9 28.8 %copy-start.28 = (f32[1024]{0:T(1024)S(1)}, f32[1024]{0:T(1024)}, u32[]{:S(2)}) copy-start(f32[1024]{0:T(1024)} %get-tuple-element.321) | copy-start | bytes 12292
  853.9 28.8 %copy-start.39 = (f32[64]{0:T(128)S(1)}, f32[64]{0:T(128)}, u32[]{:S(2)}) copy-start(f32[64]{0:T(128)} %get-tuple-element.318) | copy-start | bytes 772
  853.9 110.5 %copy-start.6 = (f32[64,1024]{1,0:T(8,128)S(1)}, f32[64,1024]{1,0:T(8,128)}, u32[]{:S(2)}) copy-start(f32[64,1024]{1,0:T(8,128)} %copy-done.5) | copy-start | bytes 786436
  853.9 110.5 %copy-start.9 = (f32[8,8,4,256]{3,1,2,0:T(8,128)S(1)}, f32[8,8,4,256]{3,1,2,0:T(8,128)}, u32[]{:S(2)}) copy-start(f32[8,8,4,256]{3,1,2,0:T(8,128)} %copy-done.8) | copy-start | bytes 786436
  853.9 110.5 %copy-start.22 = (bf16[64,1024]{1,0:T(8,128)(2,1)S(1)}, bf16[64,1024]{1,0:T(8,128)(2,1)}, u32[]{:S(2)}) copy-start(bf16[64,1024]{1,0:T(8,128)(2,1)} %param.20) | copy-start | bytes 393220
  853.9 110.5 %copy-start.30 = (f32[64]{0:T(128)S(1)}, f32[64]{0:T(128)}, u32[]{:S(2)}) copy-start(f32[64]{0:T(128)} %copy-done.29) | copy-start | bytes 772
  853.9 110.5 %copy-start.38 = (f32[64]{0:T(128)S(1)}, f32[64]{0:T(128)}, u32[]{:S(2)}) copy-start(f32[64]{0:T(128)} %copy-done.37) | copy-start | bytes 772
  997.0 9.2 copy-start.20
  1003.7 3.5 copy-start.19
Sparse Core Ops, SparseCore 0:
  11.4 63.1 all-gather.8
  78.0 59.2 reduce-scatter.11
  155.1 97.2 reduce-scatter.13
  255.6 58.9 all-gather.10
  317.3 59.2 all-gather.12
  378.7 84.0 reduce-scatter.17
  465.2 85.7 reduce-scatter.15
  555.8 50.4 all-gather.14
  608.5 48.7 all-gather.16
  661.0 26.6 reduce-scatter.21
  702.9 58.5 all-gather.18
  797.7 35.8 all-gather.20
  837.0 26.7 reduce-scatter.23
  866.0 98.3 reduce-scatter.19
  968.7 28.2 all-reduce.5
where the time goes:
time: 1020 us; the launch traced here: 1010 us
  waiting for transfers between devices  804 us (79%)
  blocking collectives  73.5 us (7%)
  matrix products  60.2 us (6%)
  local copies, waits for them, and re-layouts  39.4 us (4%)
  other arithmetic  19.2 us (2%)
  between operations  14.6 us (1%)
    all_gather x4, waiting for transfers between devices, gather_rows(): return lax.all_gather(values, ('row', 'col'), axis=0, tiled=True)  231 us
    reduce_scatter x2, waiting for transfers between devices, project_rows(): lax.psum_scatter(jnp.dot(left_rows, right_matrix, preferred_element_type=...  137 us
    reduce_scatter x1, waiting for transfers between devices, shards(): lax.psum_scatter(gate_part, 'col', scatter_dimension=1, tiled=True)  88.1 us
    reduce_scatter x1, waiting for transfers between devices, shards(): lax.psum_scatter(up_part, 'col', scatter_dimension=1, tiled=True)  86.3 us
    reduce_scatter x1, waiting for transfers between devices, shards(): lax.psum_scatter(partial_value, 'col', scatter_dimension=1, tiled=True)  58.5 us
    all_gather x1, waiting for transfers between devices, shards(): lax.all_gather(gate_low, 'col', axis=1, tiled=True)  49.9 us
    all_gather x1, waiting for transfers between devices, shards(): lax.all_gather(up_low, 'col', axis=1, tiled=True)  48.3 us
    psum x1, blocking collectives, shards(): lax.psum((attn_gain_grad, query_gain, key_gain, ffn_gain_grad), ('dp', 'r...  41.9 us
  transfers between devices with their start and end apart: 15, of which 15 were waited for; matrix products, arithmetic and copies ran while one was open for 3% of the time, Pallas kernels for 0%

commit v1 on v0

--- a/solution.py
+++ b/solution.py
@@ -3,6 +3,8 @@
 import jax
 import jax.numpy as jnp
 from jax import lax
+from jax.experimental import pallas as pl
+from jax.experimental.pallas import tpu as pltpu
 from jax.sharding import PartitionSpec as P
 
 EPSILON = 1e-05
@@ -179,26 +181,251 @@
     )
 
 
-def gather_rows(values):
-    return lax.all_gather(values, ("row", "col"), axis=0, tiled=True)
-
-
-def project_rows(left_rows, right_matrix):
-    return lax.psum_scatter(
-        jnp.dot(left_rows, right_matrix, preferred_element_type=jnp.float32),
-        ("row", "col"),
-        scatter_dimension=0,
-        tiled=True,
-    )
-
-
-def back_sum(partial_value, local_rows):
-    row_count = lax.axis_size("row")
-    col_count = lax.axis_size("col")
-    shaped = partial_value.reshape(row_count, col_count, local_rows, partial_value.shape[1])
-    summed = lax.psum_scatter(shaped, "row", scatter_dimension=0, tiled=True)
-    swapped = lax.all_to_all(summed, "col", split_axis=1, concat_axis=3, tiled=True)
-    return swapped.reshape(local_rows, -1)
+MESH = pl.DeviceIdType.MESH
+
+
+def enter(axes):
+    barrier = pltpu.get_barrier_semaphore()
+    count = 0
+    for axis in axes:
+        size, own = lax.axis_size(axis), lax.axis_index(axis)
+        for step in range(1, size):
+            pl.semaphore_signal(
+                barrier, inc=1, device_id={axis: lax.rem(own + step, size)}, device_id_type=MESH
+            )
+        count += size - 1
+    pl.semaphore_wait(barrier, count)
+
+
+def send(source, target, sems, place, axis, index):
+    copy = pltpu.make_async_remote_copy(
+        src_ref=source,
+        dst_ref=target,
+        send_sem=sems[0].at[place],
+        recv_sem=sems[1].at[place],
+        device_id={axis: index},
+        device_id_type=MESH,
+    )
+    copy.start()
+    return copy
+
+
+def start_swaps(ins, outs, sems):
+    cols, own = lax.axis_size("col"), lax.axis_index("col")
+    copies = []
+    for number in range(len(ins)):
+        for step in range(1, cols):
+            peer = lax.rem(own + step, cols)
+            copies.append(
+                send(ins[number].at[peer], outs[number].at[own], sems, (number, step), "col", peer)
+            )
+        outs[number][own] = ins[number][own]
+    return copies
+
+
+def call_kernel(body, args, outs, scratch, number):
+    vmem = pl.BlockSpec(memory_space=pltpu.VMEM)
+    return pl.pallas_call(
+        body,
+        out_shape=outs,
+        in_specs=[vmem] * len(args),
+        out_specs=[vmem] * len(outs),
+        scratch_shapes=scratch,
+        compiler_params=pltpu.CompilerParams(collective_id=number, has_side_effects=True),
+    )(*args)
+
+
+def dma(*shape):
+    return [pltpu.SemaphoreType.DMA(shape), pltpu.SemaphoreType.DMA(shape)]
+
+
+def exchange(gathers, swaps, number):
+    rows, cols = lax.axis_size("row"), lax.axis_size("col")
+    many, total = len(gathers), len(gathers) + len(swaps)
+
+    def body(*refs):
+        ins, outs = refs[:total], refs[total : 2 * total]
+        sems, swap_sems = refs[2 * total : 2 * total + 2], refs[2 * total + 2 :]
+        row, col = lax.axis_index("row"), lax.axis_index("col")
+        enter(("row", "col"))
+        across, copies = {}, []
+        for item in range(many):
+            for step in range(1, cols):
+                across[item, step] = send(
+                    ins[item],
+                    outs[item].at[row, col],
+                    sems,
+                    (item, 0, step),
+                    "col",
+                    lax.rem(col + step, cols),
+                )
+        for item in range(many):
+            for turn in range(1, rows):
+                copies.append(
+                    send(
+                        ins[item],
+                        outs[item].at[row, col],
+                        sems,
+                        (item, turn, 0),
+                        "row",
+                        lax.rem(row + turn, rows),
+                    )
+                )
+        copies += start_swaps(ins[many:], outs[many:], swap_sems)
+        for item in range(many):
+            outs[item][row, col] = ins[item][...]
+        for step in range(1, cols):
+            origin = lax.rem(col + cols - step, cols)
+            for item in range(many):
+                across[item, step].wait()
+                block = outs[item].at[row, origin]
+                for turn in range(1, rows):
+                    copies.append(
+                        send(
+                            block,
+                            block,
+                            sems,
+                            (item, turn, step),
+                            "row",
+                            lax.rem(row + turn, rows),
+                        )
+                    )
+        for copy in copies:
+            copy.wait()
+
+    outs = [jax.ShapeDtypeStruct((rows, cols) + g.shape, g.dtype) for g in gathers]
+    outs += [jax.ShapeDtypeStruct(w.shape, w.dtype) for w in swaps]
+    scratch = dma(many, rows, cols) + dma(max(len(swaps), 1), cols)
+    return call_kernel(body, list(gathers) + list(swaps), outs, scratch, number)
+
+
+def reduce_rows(partial_value, swaps, number):
+    rows, cols = lax.axis_size("row"), lax.axis_size("col")
+    local = partial_value.shape[0] // (rows * cols)
+    width = partial_value.shape[1]
+    shaped = partial_value.astype(jnp.bfloat16).reshape(rows, cols, local, width)
+    many = len(swaps)
+
+    def body(*refs):
+        part, ins = refs[0], refs[1 : 1 + many]
+        result, outs = refs[1 + many], refs[2 + many : 2 + 2 * many]
+        first, staged, second = refs[2 + 2 * many : 5 + 2 * many]
+        first_sems, second_sems = refs[5 + 2 * many : 7 + 2 * many], refs[7 + 2 * many : 9 + 2 * many]
+        swap_sems = refs[9 + 2 * many :]
+        row, col = lax.axis_index("row"), lax.axis_index("col")
+        enter(("row", "col"))
+        down, across = {}, []
+        order = list(range(1, cols)) + [0]
+        for step in order:
+            block = lax.rem(col + step, cols)
+            for turn in range(1, rows):
+                peer = lax.rem(row + turn, rows)
+                down[step, turn] = send(
+                    part.at[peer, block],
+                    first.at[turn, step],
+                    first_sems,
+                    (turn, step),
+                    "row",
+                    peer,
+                )
+        copies = start_swaps(ins, outs, swap_sems)
+        for step in order:
+            block = lax.rem(col + step, cols)
+            summed = part[row, block].astype(jnp.float32)
+            for turn in range(1, rows):
+                down[step, turn].wait()
+                summed = summed + first[turn, step].astype(jnp.float32)
+            if step == 0:
+                result[...] = summed
+            else:
+                staged[step] = summed.astype(jnp.bfloat16)
+                across.append(
+                    send(staged.at[step], second.at[step], second_sems, (step,), "col", block)
+                )
+        for step in range(1, cols):
+            across[step - 1].wait()
+            result[...] += second[step].astype(jnp.float32)
+        for copy in copies:
+            copy.wait()
+
+    outs = [jax.ShapeDtypeStruct((local, width), jnp.float32)]
+    outs += [jax.ShapeDtypeStruct(w.shape, w.dtype) for w in swaps]
+    scratch = [
+        pltpu.VMEM((rows, cols, local, width), jnp.bfloat16),
+        pltpu.VMEM((cols, local, width), jnp.bfloat16),
+        pltpu.VMEM((cols, local, width), jnp.bfloat16),
+    ]
+    scratch += dma(rows, cols) + dma(cols) + dma(max(many, 1), cols)
+    return call_kernel(body, [shaped] + list(swaps), outs, scratch, number)
+
+
+def last_sums(group_value, gains, number):
+    sizes = [lax.axis_size(axis) for axis in ("dp", "row", "col")]
+
+    def body(value, gain, value_out, gain_out, value_in, landed, held, *sems):
+        value_sems, gain_sems = sems[:2], sems[2:]
+        enter(("dp", "row", "col"))
+        copies, groups = [], lax.axis_size("dp")
+        me = lax.axis_index("dp")
+        for step in range(1, groups):
+            copies.append(
+                send(
+                    value,
+                    value_in.at[step],
+                    value_sems,
+                    (step,),
+                    "dp",
+                    lax.rem(me + step, groups),
+                )
+            )
+        held[0] = gain[...]
+        for stage, axis in enumerate(("dp", "row", "col")):
+            size, own = lax.axis_size(axis), lax.axis_index(axis)
+            sent = [
+                send(
+                    held.at[stage],
+                    landed.at[stage, step],
+                    gain_sems,
+                    (stage, step),
+                    axis,
+                    lax.rem(own + step, size),
+                )
+                for step in range(1, size)
+            ]
+            held[stage + 1] = held[stage]
+            landed[stage, 0] = held[stage]
+            for copy in sent:
+                copy.wait()
+            total = None
+            for place in range(size):
+                term = landed[stage, lax.rem(own - place + size, size)]
+                total = term if total is None else total + term
+            held[stage + 1] = total
+        gain_out[...] = held[3]
+        for copy in copies:
+            copy.wait()
+        total = value[...]
+        for step in range(1, groups):
+            total = total + value_in[step]
+        value_out[...] = total
+
+    outs = [jax.ShapeDtypeStruct(v.shape, jnp.float32) for v in (group_value, gains)]
+    scratch = [
+        pltpu.VMEM((sizes[0],) + group_value.shape, jnp.float32),
+        pltpu.VMEM((3, max(sizes)) + gains.shape, jnp.float32),
+        pltpu.VMEM((4,) + gains.shape, jnp.float32),
+    ]
+    scratch += dma(sizes[0]) + dma(3, max(sizes))
+    return call_kernel(body, [group_value, gains], outs, scratch, number)
+
+
+def dot(left, right, left_dim=1, right_dim=0):
+    return lax.dot_general(
+        left,
+        right,
+        (((left_dim,), (right_dim,)), ((), ())),
+        preferred_element_type=jnp.float32,
+    )
 
 
 def shards(
@@ -217,74 +444,89 @@
     up_weight,
     down_weight,
 ):
-    local_rows = block_input.shape[0]
+    local_rows, width = block_input.shape
     head_dim = query_norm.shape[0]
     col_width = query_weight.shape[0]
-    col_index = lax.axis_index("col")
-    slot_count = query_weight.shape[1] // head_dim
+    cols = lax.axis_size("col")
+    length = local_rows * cols * lax.axis_size("row")
+    place = (lax.axis_index("row") * cols + lax.axis_index("col")) * local_rows
+
+    def own_rows(values):
+        return lax.dynamic_slice_in_dim(values, place, local_rows, 0)
+
+    out_weight_full = lax.all_gather(out_weight, ("row", "col"), axis=0, tiled=True)
+    out_full = lax.all_gather(out_grad, ("row", "col"), axis=0, tiled=True)
+
+    query_slots = query_weight.reshape(col_width, cols, head_dim)
+    key_slots = jnp.repeat(key_weight.reshape(col_width, cols // 2, head_dim), 2, axis=1)
+    value_slots = jnp.repeat(value_weight.reshape(col_width, cols // 2, head_dim), 2, axis=1)
+    slots = jnp.concatenate([query_slots, key_slots, value_slots], axis=2).transpose(1, 0, 2)
+    hidden_width = gate_weight.shape[1] // cols
+    wide = jnp.concatenate(
+        [
+            gate_weight.reshape(col_width, cols, hidden_width),
+            up_weight.reshape(col_width, cols, hidden_width),
+        ],
+        axis=2,
+    ).transpose(1, 0, 2)
+
+    input_blocks, slot_blocks = exchange([block_input], [slots], 0)
+    input_full = input_blocks.reshape(length, width).astype(jnp.float32)
+    slot_weight = slot_blocks.reshape(width, 3 * head_dim)
+    first_full = head_norm(input_full, attn_norm)[0].astype(jnp.bfloat16)
     residual = block_input.astype(jnp.float32)
-    normed_in, scale_in = head_norm(residual, attn_norm)
-    first_act = normed_in.astype(jnp.bfloat16)
-    first_full = gather_rows(first_act)
-    length = first_full.shape[0]
-    first_cols = lax.dynamic_slice_in_dim(first_full, col_index * col_width, col_width, 1)
+    scale_in = head_norm(residual, attn_norm)[1]
     segment, position = segment_info(seq_lengths[0], length)
     cosine, sine = rope_tables(position, head_dim)
-    query_slots = query_weight.reshape(col_width, slot_count, head_dim)
-    key_slots = jnp.repeat(key_weight.reshape(col_width, slot_count // 2, head_dim), 2, axis=1)
-    value_slots = jnp.repeat(value_weight.reshape(col_width, slot_count // 2, head_dim), 2, axis=1)
-    slot_weight = jnp.stack([query_slots, key_slots, value_slots], axis=2).reshape(
-        col_width, slot_count * 3 * head_dim
-    )
-    partial_value = jnp.dot(first_cols, slot_weight, preferred_element_type=jnp.float32).reshape(
-        length, slot_count, 3 * head_dim
-    )
-    own_sums = lax.psum_scatter(partial_value, "col", scatter_dimension=1, tiled=True)[:, 0, :]
+    own_sums = dot(first_full, slot_weight)
     query_raw = own_sums[:, :head_dim]
     key_raw = own_sums[:, head_dim : 2 * head_dim]
     value_raw = own_sums[:, 2 * head_dim :]
     attn_low, log_total = head_forward(
         query_raw, key_raw, value_raw, query_norm, key_norm, cosine, sine, segment
     )
-    middle = residual + project_rows(attn_low, out_weight)
+    cat_blocks, wide_blocks = exchange([attn_low.T], [wide], 1)
+    cat_full = cat_blocks.reshape(width, length)
+    wide_weight = wide_blocks.reshape(width, 2 * hidden_width)
+    middle = input_full + dot(cat_full, out_weight_full, 0, 0)
     normed_mid, scale_mid = head_norm(middle, ffn_norm)
-    second_act = normed_mid.astype(jnp.bfloat16)
-    second_full = gather_rows(second_act)
-    second_cols = lax.dynamic_slice_in_dim(second_full, col_index * col_width, col_width, 1)
-    gate_part = jnp.dot(second_cols, gate_weight, preferred_element_type=jnp.float32)
-    up_part = jnp.dot(second_cols, up_weight, preferred_element_type=jnp.float32)
-    gating, upward = (
-        lax.psum_scatter(gate_part, "col", scatter_dimension=1, tiled=True),
-        lax.psum_scatter(up_part, "col", scatter_dimension=1, tiled=True),
-    )
+    second_full = normed_mid.astype(jnp.bfloat16)
+    wide_sums = dot(second_full, wide_weight)
+    gating, upward = wide_sums[:, :hidden_width], wide_sums[:, hidden_width:]
     sigmoid_gate = jax.nn.sigmoid(gating)
     activated = gating * sigmoid_gate
     hidden = (activated * upward).astype(jnp.bfloat16)
-    result_sum = middle + project_rows(hidden, down_weight)
-    block_output = result_sum.astype(jnp.bfloat16)
-    out_full = gather_rows(out_grad)
-    grad_down = jnp.dot(hidden.T, out_full, preferred_element_type=jnp.float32)
-    hidden_grad = jnp.dot(out_full, down_weight.T, preferred_element_type=jnp.float32)
+    hidden_grad = dot(out_full, down_weight, 1, 1)
     gate_low = (hidden_grad * upward * sigmoid_gate * (1.0 + gating * (1.0 - sigmoid_gate))).astype(
         jnp.bfloat16
     )
     up_low = (hidden_grad * activated).astype(jnp.bfloat16)
-    gate_full, up_full = (
-        lax.all_gather(gate_low, "col", axis=1, tiled=True),
-        lax.all_gather(up_low, "col", axis=1, tiled=True),
-    )
-    grad_gate = jnp.dot(second_cols.T, gate_full, preferred_element_type=jnp.float32)
-    grad_up = jnp.dot(second_cols.T, up_full, preferred_element_type=jnp.float32)
-    act_part = jnp.dot(gate_full, gate_weight.T, preferred_element_type=jnp.float32) + jnp.dot(
-        up_full, up_weight.T, preferred_element_type=jnp.float32
-    )
-    act_grad2 = back_sum(act_part, local_rows)
-    middle_back, ffn_gain_grad = head_norm_back(act_grad2, middle, scale_mid, ffn_norm)
+    wide_low = jnp.concatenate([gate_low, up_low], axis=1)
+    (act_grad2,) = reduce_rows(dot(wide_low, wide_weight, 1, 1), [], 2)
+    down_sums = lax.psum_scatter(
+        dot(hidden, down_weight), ("row", "col"), scatter_dimension=0, tiled=True
+    )
+    middle_own = own_rows(middle)
+    block_output = (middle_own + down_sums).astype(jnp.bfloat16)
+    grad_down = dot(hidden, out_full, 0, 0)
+    wide_grad = dot(second_full, wide_low, 0, 0).astype(jnp.bfloat16)
+    middle_back, ffn_gain_grad = head_norm_back(
+        act_grad2, middle_own, own_rows(scale_mid), ffn_norm
+    )
     middle_grad = out_grad.astype(jnp.float32) + middle_back
-    middle_full = gather_rows(middle_grad.astype(jnp.bfloat16))
-    grad_outweight = jnp.dot(attn_low.T, middle_full, preferred_element_type=jnp.float32)
-    cat_grad = jnp.dot(middle_full, out_weight.T, preferred_element_type=jnp.float32).astype(
-        jnp.bfloat16
+    middle_blocks, wide_grads = exchange(
+        [middle_grad.astype(jnp.bfloat16)],
+        [wide_grad.reshape(cols, col_width, 2 * hidden_width)],
+        3,
+    )
+    middle_full = middle_blocks.reshape(length, width)
+    grad_outweight = dot(attn_low, middle_full, 0, 0)
+    cat_grad = dot(middle_full, out_weight, 1, 1).astype(jnp.bfloat16)
+    wide_grads = wide_grads.astype(jnp.float32).transpose(1, 0, 2)
+    grad_gate = wide_grads[:, :, :hidden_width].reshape(col_width, -1)
+    grad_up = wide_grads[:, :, hidden_width:].reshape(col_width, -1)
+    grad_outweight, grad_gate, grad_up, grad_down = lax.psum(
+        (grad_outweight, grad_gate, grad_up, grad_down), "dp"
     )
     query_low, key_low, value_low, query_gain, key_gain = head_backward(
         query_raw,
@@ -299,42 +541,40 @@
         cat_grad,
         log_total,
     )
-    own_slot = jnp.concatenate([query_low, key_low, value_low], axis=1)[:, None, :]
-    all_slots = lax.all_gather(own_slot, "col", axis=1, tiled=True).reshape(
-        length, slot_count * 3 * head_dim
-    )
-    act_grad1 = back_sum(
-        jnp.dot(all_slots, slot_weight.T, preferred_element_type=jnp.float32), local_rows
-    )
-    slot_grad = jnp.dot(first_cols.T, all_slots, preferred_element_type=jnp.float32).reshape(
-        col_width, slot_count, 3, head_dim
-    )
-    grad_query = slot_grad[:, :, 0].reshape(col_width, slot_count * head_dim)
-    grad_key = jnp.sum(
-        slot_grad[:, :, 1].reshape(col_width, slot_count // 2, 2, head_dim), axis=2
-    ).reshape(col_width, -1)
-    grad_value = jnp.sum(
-        slot_grad[:, :, 2].reshape(col_width, slot_count // 2, 2, head_dim), axis=2
-    ).reshape(col_width, -1)
+    own_slot = jnp.concatenate([query_low, key_low, value_low], axis=1)
+    slot_grad = dot(first_full, own_slot, 0, 0).astype(jnp.bfloat16)
+    act_grad1, slot_grads = reduce_rows(
+        dot(own_slot, slot_weight, 1, 1),
+        [slot_grad.reshape(cols, col_width, 3 * head_dim)],
+        4,
+    )
+    slot_grads = slot_grads.astype(jnp.float32)
+    query_part = slot_grads[:, :, :head_dim].transpose(1, 0, 2).reshape(col_width, -1)
+    pairs = slot_grads.reshape(cols // 2, 2, col_width, 3 * head_dim).sum(axis=1).transpose(1, 0, 2)
+    key_part = pairs[:, :, head_dim : 2 * head_dim].reshape(col_width, -1)
+    value_part = pairs[:, :, 2 * head_dim :].reshape(col_width, -1)
     input_back, attn_gain_grad = head_norm_back(act_grad1, residual, scale_in, attn_norm)
     input_grad = middle_grad + input_back
-    grad_query, grad_key, grad_value, grad_outweight, grad_gate, grad_up, grad_down = lax.psum(
-        (grad_query, grad_key, grad_value, grad_outweight, grad_gate, grad_up, grad_down), "dp"
-    )
-    grad_attnnorm, grad_qnorm, grad_knorm, grad_ffnnorm = lax.psum(
-        (attn_gain_grad, query_gain, key_gain, ffn_gain_grad), ("dp", "row", "col")
-    )
+    head_gains = jnp.concatenate(
+        [query_gain, key_gain, jnp.zeros((width - 2 * head_dim,), jnp.float32)]
+    )
+    gains = jnp.stack([attn_gain_grad, ffn_gain_grad, head_gains])
+    gains = jnp.concatenate([gains, jnp.zeros((5, width), jnp.float32)], axis=0)
+    group_sums, gain_sums = last_sums(
+        jnp.concatenate([query_part, key_part, value_part], axis=1), gains, 5
+    )
+    query_width, key_width = query_part.shape[1], key_part.shape[1]
     return (
         block_output,
         input_grad,
-        grad_attnnorm,
-        grad_query,
-        grad_key,
-        grad_value,
-        grad_qnorm,
-        grad_knorm,
+        gain_sums[0],
+        group_sums[:, :query_width],
+        group_sums[:, query_width : query_width + key_width],
+        group_sums[:, query_width + key_width :],
+        gain_sums[2, :head_dim],
+        gain_sums[2, head_dim : 2 * head_dim],
         grad_outweight,
-        grad_ffnnorm,
+        gain_sums[1],
         grad_gate,
         grad_up,
         grad_down,

time: 1020 us -> 422 us (0.41)
  waiting for transfers between devices: 804 us -> 17.7 us
  Pallas kernels: 0 us -> 229 us
  blocking collectives: 73.5 us -> 0 us
  local copies, waits for them, and re-layouts: 39.4 us -> 69.4 us
  other arithmetic: 19.2 us -> 30.3 us
    reduce_scatter x5 -> x1, waiting for transfers between devices: 370 us -> 7.39 us  [shards(): lax.psum_scatter(dot(hidden, down_weight), ('row', 'col'), scatter_dimens...]
    all_gather x7 -> x2, waiting for transfers between devices: 365 us -> 8.92 us  [the longest x1 8.89 us: shards(): out_full = lax.all_gather(out_grad, ('row', 'col'), axis=0, tiled=True)]
    pallas_call x0 -> x6, Pallas kernels: none -> 229 us  [call_kernel(): pl.pallas_call(body, out_shape=outs, in_specs=[vmem] * len(args), out_spe...]
    psum x1 -> x0, blocking collectives: 41.9 us -> none  [shards(): lax.psum((attn_gain_grad, query_gain, key_gain, ffn_gain_grad), ('dp', 'r...]
    unnamed x17 -> x4, waiting for transfers between devices: 38.2 us -> 1.41 us
    all_to_all x2 -> x0, blocking collectives: 31.6 us -> none  [back_sum(): lax.all_to_all(summed, 'col', split_axis=1, concat_axis=3, tiled=True)]
    psum x1, waiting for transfers between devices: 30.7 us -> 0.01 us  [shards(): lax.psum((grad_outweight, grad_gate, grad_up, grad_down), 'dp')]
    slice x1 -> x9, local copies, waits for them, and re-layouts: 0.05 us -> 13.1 us  [the longest x2 5.11 us: shards(): grad_up = wide_grads[:, :, hidden_width:].reshape(col_width, -1)]
  transfers between devices with their start and end apart: 15 -> 4, of which waited for: 15 -> 2; matrix products, arithmetic and copies ran while one was open for 3% -> 27% of each run, Pallas kernels for 0% -> 38%
where the time goes in v1:
time: 422 us; the launch traced here: 420 us
  Pallas kernels  229 us (54%)
  local copies, waits for them, and re-layouts  69.4 us (16%)
  matrix products  56.1 us (13%)
  other arithmetic  30.3 us (7%)
  waiting for transfers between devices  17.7 us (4%)
  between operations  14.4 us (3%)
    pallas_call x6, Pallas kernels, call_kernel(): pl.pallas_call(body, out_shape=outs, in_specs=[vmem] * len(args), out_spe...  229 us
    dot_general x12, matrix products, dot(): lax.dot_general(left, right, (((left_dim,), (right_dim,)), ((), ())), pre...  34.1 us
    unnamed x94, local copies, waits for them, and re-layouts  24.9 us
    all_gather x1, waiting for transfers between devices, shards(): out_full = lax.all_gather(out_grad, ('row', 'col'), axis=0, tiled=True)  8.89 us
  transfers between devices with their start and end apart: 4, of which 2 were waited for; matrix products, arithmetic and copies ran while one was open for 27% of the time, Pallas kernels for 38%

profile of v1, /device:TPU:0, one launch (start us, length us, event | category | flops | bytes accessed | tf_op | source)
XLA Modules:
  0.0 419.9 jit_solution(5925742317390431561)
XLA Ops:
  13.2 36.4 %shard_map.237 = (bf16[4,4,64,1024]{3,2,1,0:T(8,128)(2,1)}, bf16[4,256,192]{2,1,0:T(8,128)(2,1)}) custom-call(bf16[64,1024]{1,0:T(8,128)(2,1)} %refs_0_.1, bf16[4,256,192]{2,1,0:T(8,128)(2,1)} %maximum_bitcast_fusion.1.refs_1_), custom_call_target="tpu_custom_call" | custom-call | tf_op jit(solution)/shard_map/pallas_call | solution.py:228
  49.6 2.2 fusion.16
  56.0 1.8 fusion.54
  58.5 1.7 copy.110
  60.2 1.5 pad_maximum_fusion.10
  61.7 1.7 copy.111
  63.5 1.7 copy.112
  65.2 11.0 %while.28 = (s32[]{:T(128)}, bf16[2,512,64]{1,2,0:T(8,128)(2,1)}, f32[2,512]{1,0:T(2,128)}, s32[2]{0:T(128)S(1)}, s32[1024]{0:T(1024)S(1)}, /*index=5*/bf16[1024...) while((s32[]{:T(128)}, bf16[2,512,64]{1,2,0:T(8,128)(2,1)}, ...), condition=%wide.region_8.9_spmd.clone, body=%wide.region_6.8_spmd.clone.sunk | while | flops 141033472 | bytes 6621527 | solution.py:85
  66.6 1.9 select_reduce_fusion.3
  72.0 1.9 select_reduce_fusion.3
  76.2 1.6 copy.154
  77.7 2.1 copy.115
  79.9 2.2 copy.117
  82.1 2.1 copy.114
  84.2 2.2 copy.116
  86.4 2.9 maximum_bitcast_fusion.refs_1_
  89.3 48.0 %shard_map.238 = (bf16[4,4,64,1024]{3,2,1,0:T(8,128)(2,1)}, bf16[4,256,576]{2,1,0:T(8,128)(2,1)}) custom-call(bf16[64,1024]{1,0:T(8,128)(2,1)} %bitcast.12.refs_0_, bf16[4,256,576]{2,1,0:T(8,128)(2,1)} %maximum_bitcast_fusion.refs_1_), custom_call_target="tpu_custom_call" | custom-call | tf_op jit(solution)/shard_map/pallas_call | solution.py:228
  137.4 5.3 %multiply_reduce_fusion.1 = (f32[1024]{0:T(1024)S(1)}, f32[1024,1024]{1,0:T(8,128)S(1)}) fusion(bf16[1024,1024]{1,0:T(8,128)(2,1)} %bitcast.167, bf16[1024,1024]{1,0:T(8,128)(2,1)} %all-gather.3.cloned.1.call-done, bf16[4,4,64,1024]{3,2,1,0:T(8,128)(2,1)S(1)} %copy-done.1), kind=kOutput, calls=%fused_computation.39 | convolution fusion | flops 2151676928 | bytes 10489856 | tf_op jit(solution)/shard_map/dot_general | solution.py:423
  142.7 1.9 copy-done.4
  144.6 3.1 fusion.66
  147.7 8.9 %all-gather.5.cloned.1.call-done = bf16[1024,1024]{1,0:T(8,128)(2,1)} async-done(((bf16[64,1024]{1,0:T(8,128)(2,1)}), bf16[1024,1024]{1,0:T(8,128)(2,1)}) %all-gather.5.cloned.1.call-update) | async-done | bytes 2097168 | tf_op jit(solution)/shard_map/all_gather | solution.py:458
  156.6 4.4 %multiply_convert_fusion.3 = (bf16[1024,288]{0,1:T(8,128)(2,1)S(1)}, bf16[1024,288]{0,1:T(8,128)(2,1)S(1)}, bf16[1024,288]{0,1:T(8,128)(2,1)}) fusion(f32[1024,576]{0,1:T(8,128)} %fusion.66, bf16[1024,1024]{1,0:T(8,128)(2,1)} %all-gather.5.cloned.1.call-done, bf16[288,1024]{1,0:T(8,128)(2,1)S(1)} %copy-done), kind=kOutput, calls=%fused_computation.48 | convolution fusion | flops 608403456 | bytes 6815744 | tf_op jit(solution)/shard_map/dot_general | solution.py:423
  161.0 3.1 convolution_convert_fusion.1
  164.1 2.5 convolution_convert_fusion.2
  166.7 28.6 %shard_map.239 = f32[64,1024]{1,0:T(8,128)} custom-call(bf16[4,4,64,1024]{3,2,1,0:T(8,128)(2,1)} %bitcast.140), custom_call_target="tpu_custom_call" | custom-call | tf_op jit(solution)/shard_map/pallas_call | solution.py:228
  195.4 1.7 multiply_reduce_fusion.4
  197.1 1.8 fusion.65.refs_0_
  199.0 2.4 copy.118
  201.4 39.5 %shard_map.240 = (bf16[4,4,64,1024]{3,2,1,0:T(8,128)(2,1)}, bf16[4,256,576]{2,1,0:T(8,128)(2,1)}) custom-call(bf16[64,1024]{1,0:T(8,128)(2,1)} %fusion.65.refs_0_, bf16[4,256,576]{2,1,0:T(8,128)(2,1)} %bitcast.134), custom_call_target="tpu_custom_call" | custom-call | tf_op jit(solution)/shard_map/pallas_call | solution.py:228
  240.9 1.5 convert_bitcast_fusion
  242.4 2.2 fusion.67
  244.6 2.9 copy.132
  247.5 2.9 copy.133
  250.4 2.9 fusion.73
  253.3 3.4 fusion.74
  256.7 4.4 %fusion.72 = f32[1024,1024]{1,0:T(8,128)} fusion(bf16[1024,288]{0,1:T(8,128)(2,1)} %get-tuple-element.401, bf16[288,1024]{1,0:T(8,128)(2,1)S(1)} %copy-done), kind=kOutput, calls=%fused_computation.151 | convolution fusion | flops 603979776 | bytes 5373952 | tf_op jit(solution)/shard_map/dot_general | solution.py:423
  264.7 1.9 fusion.20
  266.6 1.4 convolution_convert_fusion.4
  268.5 31.9 %while.29 = (s32[]{:T(128)}, f32[1024,64]{0,1:T(8,128)}, f32[1024,64]{0,1:T(8,128)}, f32[2,512,64]{1,0,2:T(2,128)}, s32[2]{0:T(128)}, /*index=5*/s32[1024]{0:T(1...) while((s32[]{:T(128)}, f32[1024,64]{0,1:T(8,128)}, ...), condition=%wide.region_15.16_spmd.clone, body=%wide.region_13.15_spmd.clone.sunk | while | flops 342228992 | bytes 9593086 | solution.py:128
  268.5 1.3 dynamic_slice.79
  271.3 1.9 select_convert_fusion.6
  274.5 1.5 multiply_convert_fusion.10
  276.0 2.0 convolution_add_fusion.4
  278.9 1.4 convolution_bitcast_fusion.3
  280.5 3.5 dynamic_update_slice.20
  284.0 1.3 dynamic_slice.79
  286.7 1.8 select_convert_fusion.6
  289.9 1.5 multiply_convert_fusion.10
  291.4 2.1 convolution_add_fusion.4
  293.4 2.0 convolution_add_fusion.5
  295.4 1.4 convolution_bitcast_fusion.3
  296.9 3.5 dynamic_update_slice.20
  302.5 1.6 fusion.57
  306.9 2.1 convolution_convert_fusion
  308.9 51.9 %shard_map.241 = (f32[64,1024]{1,0:T(8,128)}, bf16[4,256,192]{2,1,0:T(8,128)(2,1)}) custom-call(bf16[4,4,64,1024]{3,2,1,0:T(8,128)(2,1)} %bitcast.132, bf16[4,256,192]{2,1,0:T(8,128)(2,1)} %bitcast.139), custom_call_target="tpu_custom_call" | custom-call | tf_op jit(solution)/shard_map/pallas_call | solution.py:228
  366.1 24.6 %shard_map.242 = (f32[256,512]{1,0:T(8,128)}, f32[8,1024]{1,0:T(8,128)}) custom-call(f32[256,512]{1,0:T(8,128)} %pad_maximum_fusion.3.value, f32[8,1024]{1,0:T(8,128)} %maximum_maximum_fusion.gain), custom_call_target="tpu_custom_call" | custom-call | tf_op jit(solution)/shard_map/pallas_call | solution.py:228
  390.7 1.7 slice.97
  392.3 1.3 slice_bitcast_fusion.1
  393.7 1.4 fusion.70
  395.1 1.7 fusion.68
  396.8 2.7 copy.134
  399.5 2.8 copy.135
  402.3 7.4 %reduce-scatter.2.cloned.1.call-done = f32[64,1024]{1,0:T(8,128)} async-done(((f32[1024,1024]{1,0:T(8,128)}), f32[64,1024]{1,0:T(8,128)}) %reduce-scatter.2.cloned.1.call-update) | async-done | bytes 262160 | tf_op jit(solution)/shard_map/reduce_scatter | solution.py:506
  409.7 2.0 fusion.28
  (201 shorter events, 37.6 us)
Async XLA Ops:
  7.2 149.4 %copy-start = (bf16[288,1024]{1,0:T(8,128)(2,1)S(1)}, bf16[288,1024]{1,0:T(8,128)(2,1)}, u32[]{:S(2)}) copy-start(bf16[288,1024]{1,0:T(8,128)(2,1)} %param.31) | copy-start | bytes 1769476
  7.2 130.1 %all-gather.3.cloned.1.call-start = ((), (), s32[]{:S(2)}) async-start(), calls=%async_computation.1 | async-start | bytes 2228224 | tf_op jit(solution)/shard_map/all_gather | solution.py:457
  7.9 148.6 %all-gather.5.cloned.1.call-start = ((), (), s32[]{:S(2)}) async-start(), calls=%async_computation.3 | async-start | bytes 2228224 | tf_op jit(solution)/shard_map/all_gather | solution.py:458
  8.7 388.1 %all-reduce.3.cloned.1.call-start = ((), (), s32[]{:S(2)}) async-start(), calls=%async_computation.4 | async-start | bytes 7602176 | tf_op jit(solution)/shard_map/psum | solution.py:528
  12.1 39.7 %copy-start.44 = (s32[1,5]{1,0:T(1,128)S(1)}, s32[1,5]{1,0:T(1,128)}, u32[]{:S(2)}) copy-start(s32[1,5]{1,0:T(1,128)} %param.19) | copy-start | bytes 64
  12.2 40.0 %copy-start.26 = (f32[1024]{0:T(1024)S(1)}, f32[1024]{0:T(1024)}, u32[]{:S(2)}) copy-start(f32[1024]{0:T(1024)} %param.21) | copy-start | bytes 12292
  49.6 2.6 copy-start.1
  52.2 3.8 copy-start.29
  52.2 1.0 copy-start.9
  53.2 2.2 copy-start.31
  53.2 2.2 copy-start.33
  55.4 0.6 copy-start.22
  55.4 0.6 copy-start.24
  66.6 2.0 copy-start.2
  66.6 2.0 copy-start.19
  68.5 1.5 copy-start.37
  69.4 0.7 copy-start.20
  70.1 0.6 copy-start.38
  72.0 2.0 copy-start.2
  72.0 2.0 copy-start.19
  74.0 1.5 copy-start.37
  74.9 0.7 copy-start.20
  75.6 0.6 copy-start.38
  137.3 7.2 %copy-start.12 = (bf16[4,256,576]{2,1,0:T(8,128)(2,1)S(1)}, bf16[4,256,576]{2,1,0:T(8,128)(2,1)}, u32[]{:S(2)}) copy-start(bf16[4,256,576]{2,1,0:T(8,128)(2,1)} %get-tuple-element.144) | copy-start | bytes 3538948
  137.4 7.2 %copy-start.21 = (f32[1024]{0:T(1024)S(1)}, f32[1024]{0:T(1024)}, u32[]{:S(2)}) copy-start(f32[1024]{0:T(1024)} %param.28) | copy-start | bytes 12292
  142.6 1.9 copy-start.4
  156.6 4.4 %copy-start.13 = (bf16[4,256,576]{2,1,0:T(8,128)(2,1)S(1)}, bf16[4,256,576]{2,1,0:T(8,128)(2,1)}, u32[]{:S(2)}) copy-start(bf16[4,256,576]{2,1,0:T(8,128)(2,1)} %get-tuple-element.144) | copy-start | bytes 3538948
  161.0 3.1 copy-start.5
  195.4 45.5 %copy-start.35 = (f32[64]{0:T(128)}, f32[64]{0:T(128)S(1)}, u32[]{:S(2)}) copy-start(f32[64]{0:T(128)S(1)} %dynamic-slice.3) | copy-start | bytes 772
  197.1 43.8 %copy-start.41 = (f32[64]{0:T(128)}, f32[64]{0:T(128)S(1)}, u32[]{:S(2)}) copy-start(f32[64]{0:T(128)S(1)} %broadcast_multiply_fusion.3) | copy-start | bytes 772
  250.4 2.9 copy-start.11
  256.7 153.0 %reduce-scatter.2.cloned.1.call-start = ((), (), s32[]{:S(2)}) async-start(), calls=%async_computation.2 | async-start | bytes 4456448 | tf_op jit(solution)/shard_map/reduce_scatter | solution.py:506
  261.2 0.7 copy-start.39
  261.2 3.5 copy-start.27
  264.7 1.9 copy-start.3
  264.7 1.9 copy-start.17
  268.5 35.6 %copy-start.23 = (f32[1024]{0:T(1024)S(1)}, f32[1024]{0:T(1024)}, u32[]{:S(2)}) copy-start(f32[1024]{0:T(1024)} %copy-done.22) | copy-start | bytes 12292
  268.5 35.6 %copy-start.25 = (f32[1024]{0:T(1024)S(1)}, f32[1024]{0:T(1024)}, u32[]{:S(2)}) copy-start(f32[1024]{0:T(1024)} %copy-done.24) | copy-start | bytes 12292
  300.4 4.7 %copy-start.32 = (f32[64]{0:T(128)S(1)}, f32[64]{0:T(128)}, u32[]{:S(2)}) copy-start(f32[64]{0:T(128)} %param.26) | copy-start | bytes 772
  300.4 4.7 %copy-start.34 = (f32[64]{0:T(128)S(1)}, f32[64]{0:T(128)}, u32[]{:S(2)}) copy-start(f32[64]{0:T(128)} %param.25) | copy-start | bytes 772
  301.4 3.9 copy-start.8
  305.2 1.6 copy-start.10
  363.5 1.6 copy-start.7
  363.6 1.6 copy-start.16
  363.6 1.6 copy-start.28
  363.6 1.6 copy-start.40
  363.7 1.7 copy-start.30
  363.7 1.6 copy-start.43
  396.8 12.9 %copy-start.6 = (f32[64,1024]{1,0:T(8,128)S(1)}, f32[64,1024]{1,0:T(8,128)}, u32[]{:S(2)}) copy-start(f32[64,1024]{1,0:T(8,128)} %shard_map.239) | copy-start | bytes 786436
  396.8 12.9 %copy-start.15 = (bf16[64,1024]{1,0:T(8,128)(2,1)S(1)}, bf16[64,1024]{1,0:T(8,128)(2,1)}, u32[]{:S(2)}) copy-start(bf16[64,1024]{1,0:T(8,128)(2,1)} %param.20) | copy-start | bytes 393220
  396.8 12.9 %copy-start.36 = (f32[64]{0:T(128)S(1)}, f32[64]{0:T(128)}, u32[]{:S(2)}) copy-start(f32[64]{0:T(128)} %copy-done.35) | copy-start | bytes 772
  396.8 12.9 %copy-start.42 = (f32[64]{0:T(128)S(1)}, f32[64]{0:T(128)}, u32[]{:S(2)}) copy-start(f32[64]{0:T(128)} %copy-done.41) | copy-start | bytes 772
  399.5 12.1 %copy-start.18 = (f32[64,1024]{1,0:T(8,128)S(1)}, f32[64,1024]{1,0:T(8,128)}, u32[]{:S(2)}) copy-start(f32[64,1024]{1,0:T(8,128)} %get-tuple-element.652) | copy-start | bytes 786436
  399.5 12.8 %copy-start.14 = (f32[288,1024]{1,0:T(8,128)S(1)}, f32[288,1024]{1,0:T(8,128)}, u32[]{:S(2)}) copy-start(f32[288,1024]{1,0:T(8,128)} %get-tuple-element.656) | copy-start | bytes 3538948
Sparse Core Ops, SparseCore 0:
  10.8 71.0 all-gather.2
  84.7 71.7 all-gather.4
  256.8 29.0 all-reduce.2
  288.0 121.6 reduce-scatter.1

commit v2 on v1

--- a/solution.py
+++ b/solution.py
@@ -1,3 +1,4 @@
+import functools
 import math
 
 import jax
@@ -28,24 +29,6 @@
     return (jnp.cos(angles), jnp.sin(angles))
 
 
-def rotate(values, cosine, sine):
-    half_width = values.shape[-1] // 2
-    first_half = values[:, :half_width]
-    second_half = values[:, half_width:]
-    return jnp.concatenate(
-        [first_half * cosine - second_half * sine, second_half * cosine + first_half * sine], axis=1
-    )
-
-
-def rotate_back(cotangent, cosine, sine):
-    half_width = cotangent.shape[-1] // 2
-    first_half = cotangent[:, :half_width]
-    second_half = cotangent[:, half_width:]
-    return jnp.concatenate(
-        [first_half * cosine + second_half * sine, second_half * cosine - first_half * sine], axis=1
-    )
-
-
 def head_norm(values, gain_vec):
     inv_rms = lax.rsqrt(jnp.mean(values * values, axis=-1, keepdims=True) + EPSILON)
     return (values * inv_rms * gain_vec, inv_rms)
@@ -59,126 +42,135 @@
     return (inv_rms * (weighted - normed * inner_mean), gain_grad)
 
 
-def attend(queries, key_rows, value_rows, segment):
-    length = queries.shape[0]
-    block_rows = min(512, length)
-    places = jnp.arange(length, dtype=jnp.int32)
-    score_scale = 1.0 / math.sqrt(queries.shape[1])
-
-    def one_block(number):
-        offset = number * block_rows
-        query_block = lax.dynamic_slice_in_dim(queries, offset, block_rows, 0)
-        row_segment = lax.dynamic_slice_in_dim(segment, offset, block_rows, 0)
-        row_places = offset + jnp.arange(block_rows, dtype=jnp.int32)
-        allowed = (row_segment[:, None] == segment[None, :]) & (
-            places[None, :] <= row_places[:, None]
+def swap_halves(values):
+    half_width = values.shape[-1] // 2
+    return jnp.concatenate([values[:, half_width:], values[:, :half_width]], axis=1)
+
+
+def block_probability(query_block, key_rows, begins, offset, low, shift):
+    score_scale = 1.0 / math.sqrt(query_block.shape[1])
+    scores = dot(query_block, key_rows, 1, 1) * score_scale
+    places = low + lax.broadcasted_iota(jnp.int32, scores.shape, 1)
+    row_places = offset + lax.broadcasted_iota(jnp.int32, scores.shape, 0)
+    allowed = (places >= begins) & (places <= row_places)
+    if shift is None:
+        shift = jnp.log(jnp.sum(jnp.where(allowed, jnp.exp(scores), 0.0), axis=1, keepdims=True))
+    probability = jnp.where(allowed, jnp.exp(scores - shift), 0.0).astype(jnp.bfloat16)
+    return probability, shift
+
+
+def spans(length, longest):
+    block = min(256, length)
+    return [
+        (offset, max(0, (offset - longest) // 128 * 128), block)
+        for offset in range(0, length, block)
+    ]
+
+
+def attend_kernel(longest, sums, gains, cosine, sine, begins, *outs):
+    query_rot, key_rot, value_low, low_rows, low_cols, totals = outs
+    length, head_dim = query_rot.shape
+    for place, target in ((0, query_rot), (1, key_rot)):
+        normed = head_norm(
+            sums[:, place * head_dim : (place + 1) * head_dim], gains[place : place + 1, :]
+        )[0]
+        target[...] = (normed * cosine[...] + swap_halves(normed) * sine[...]).astype(jnp.bfloat16)
+    value_low[...] = sums[:, 2 * head_dim : 3 * head_dim].astype(jnp.bfloat16)
+    for offset, low, block in spans(length, longest):
+        rows, keys = slice(offset, offset + block), slice(low, offset + block)
+        probability, total = block_probability(
+            query_rot[rows, :], key_rot[keys, :], begins[rows, :], offset, low, None
         )
-        scores = jnp.dot(query_block, key_rows.T, preferred_element_type=jnp.float32) * score_scale
-        exponent = jnp.where(allowed, jnp.exp(scores), 0.0)
-        log_total = jnp.log(jnp.sum(exponent, axis=1))
-        probability = jnp.where(allowed, jnp.exp(scores - log_total[:, None]), 0.0).astype(
-            jnp.bfloat16
+        totals[rows, :] = total
+        low_rows[rows, :] = dot(probability, value_low[keys, :]).astype(jnp.bfloat16)
+        low_cols[:, rows] = dot(value_low[keys, :], probability, 0, 1).astype(jnp.bfloat16)
+
+
+def attend_back_kernel(longest, *refs):
+    query_rot, key_rot, value_low, low_rows, totals, grads = refs[:6]
+    sums, gains, cosine, sine, begins = refs[6:11]
+    slot, gain_out, query_acc, key_acc, value_acc = refs[11:]
+    length, head_dim = query_rot.shape
+    score_scale = 1.0 / math.sqrt(head_dim)
+    key_acc[...] = jnp.zeros_like(key_acc)
+    value_acc[...] = jnp.zeros_like(value_acc)
+    for offset, low, block in spans(length, longest):
+        rows, keys = slice(offset, offset + block), slice(low, offset + block)
+        probability, _ = block_probability(
+            query_rot[rows, :], key_rot[keys, :], begins[rows, :], offset, low, totals[rows, :]
         )
-        output = jnp.dot(probability, value_rows, preferred_element_type=jnp.float32)
-        return (output, log_total)
-
-    outputs, totals = lax.map(one_block, jnp.arange(length // block_rows, dtype=jnp.int32))
-    return (outputs.reshape(length, -1), totals.reshape(length))
-
-
-def attend_back(queries, key_rows, value_rows, segment, output_rows, out_grads, log_total):
-    length = queries.shape[0]
-    block_rows = min(512, length)
-    places = jnp.arange(length, dtype=jnp.int32)
-    score_scale = 1.0 / math.sqrt(queries.shape[1])
-
-    def one_block(carried, number):
-        key_total, value_total = carried
-        offset = number * block_rows
-        query_block = lax.dynamic_slice_in_dim(queries, offset, block_rows, 0)
-        row_segment = lax.dynamic_slice_in_dim(segment, offset, block_rows, 0)
-        grad_block = lax.dynamic_slice_in_dim(out_grads, offset, block_rows, 0)
-        out_block = lax.dynamic_slice_in_dim(output_rows, offset, block_rows, 0)
-        total_block = lax.dynamic_slice_in_dim(log_total, offset, block_rows, 0)
-        row_places = offset + jnp.arange(block_rows, dtype=jnp.int32)
-        allowed = (row_segment[:, None] == segment[None, :]) & (
-            places[None, :] <= row_places[:, None]
+        grad_block = grads[rows, :]
+        value_acc[keys, :] += dot(probability, grad_block, 0, 0)
+        row_delta = jnp.sum(
+            grad_block.astype(jnp.float32) * low_rows[rows, :].astype(jnp.float32),
+            axis=1,
+            keepdims=True,
         )
-        scores = jnp.dot(query_block, key_rows.T, preferred_element_type=jnp.float32) * score_scale
-        probability = jnp.where(allowed, jnp.exp(scores - total_block[:, None]), 0.0).astype(
-            jnp.bfloat16
-        )
-        value_total = value_total + jnp.dot(
-            probability.T, grad_block, preferred_element_type=jnp.float32
-        )
-        prob_grad = jnp.dot(grad_block, value_rows.T, preferred_element_type=jnp.float32)
-        row_delta = jnp.sum(
-            grad_block.astype(jnp.float32) * out_block.astype(jnp.float32), axis=1, keepdims=True
-        )
+        prob_grad = dot(grad_block, value_low[keys, :], 1, 1)
         score_grad = (
             score_scale * probability.astype(jnp.float32) * (prob_grad - row_delta)
         ).astype(jnp.bfloat16)
-        query_grad = jnp.dot(score_grad, key_rows, preferred_element_type=jnp.float32)
-        key_total = key_total + jnp.dot(
-            score_grad.T, query_block, preferred_element_type=jnp.float32
-        )
-        return ((key_total, value_total), query_grad)
-
-    zero_rows = jnp.zeros((length, queries.shape[1]), jnp.float32)
-    (key_grad, value_grad), query_grads = lax.scan(
-        one_block, (zero_rows, zero_rows), jnp.arange(length // block_rows, dtype=jnp.int32)
-    )
-    return (query_grads.reshape(length, -1), key_grad, value_grad)
-
-
-def head_inputs(query_raw, key_raw, value_raw, query_norm, key_norm, cosine, sine):
-    query_normed, query_scale = head_norm(query_raw, query_norm)
-    key_normed, key_scale = head_norm(key_raw, key_norm)
-    query_rot = rotate(query_normed, cosine, sine).astype(jnp.bfloat16)
-    key_rot = rotate(key_normed, cosine, sine).astype(jnp.bfloat16)
-    return (query_rot, key_rot, value_raw.astype(jnp.bfloat16), query_scale, key_scale)
-
-
-def head_forward(query_raw, key_raw, value_raw, query_norm, key_norm, cosine, sine, segment):
-    query_rot, key_rot, value_low, query_scale, key_scale = head_inputs(
-        query_raw, key_raw, value_raw, query_norm, key_norm, cosine, sine
-    )
-    output, log_total = attend(query_rot, key_rot, value_low, segment)
-    return (output.astype(jnp.bfloat16), log_total)
-
-
-def head_backward(
-    query_raw,
-    key_raw,
-    value_raw,
-    query_norm,
-    key_norm,
-    cosine,
-    sine,
-    segment,
-    attn_low,
-    cat_grad,
-    log_total,
-):
-    query_rot, key_rot, value_low, query_scale, key_scale = head_inputs(
-        query_raw, key_raw, value_raw, query_norm, key_norm, cosine, sine
-    )
-    query_grad, key_grad, value_grad = attend_back(
-        query_rot, key_rot, value_low, segment, attn_low, cat_grad, log_total
-    )
-    query_pre, query_gain = head_norm_back(
-        rotate_back(query_grad, cosine, sine), query_raw, query_scale, query_norm
-    )
-    key_pre, key_gain = head_norm_back(
-        rotate_back(key_grad, cosine, sine), key_raw, key_scale, key_norm
-    )
-    return (
-        query_pre.astype(jnp.bfloat16),
-        key_pre.astype(jnp.bfloat16),
-        value_grad.astype(jnp.bfloat16),
-        query_gain,
-        key_gain,
-    )
+        query_acc[rows, :] = dot(score_grad, key_rot[keys, :])
+        key_acc[keys, :] += dot(score_grad, query_rot[rows, :], 0, 0)
+    parts = []
+    for place, source in ((0, query_acc), (1, key_acc)):
+        raw = sums[:, place * head_dim : (place + 1) * head_dim]
+        gain = gains[place : place + 1, :]
+        inv_rms = head_norm(raw, gain)[1]
+        cotangent = source[...] * cosine[...] - swap_halves(source[...]) * sine[...]
+        low_part, gain_grad = head_norm_back(cotangent, raw, inv_rms, gain)
+        parts.append(low_part.astype(jnp.bfloat16))
+        gain_out[place : place + 1, :] = gain_grad[None, :]
+    parts.append(value_acc[...].astype(jnp.bfloat16))
+    for place in range(3):
+        slot[:, place * head_dim : (place + 1) * head_dim] = parts[place]
+
+
+def local_kernel(body, args, outs, scratch=()):
+    vmem = pl.BlockSpec(memory_space=pltpu.VMEM)
+    return pl.pallas_call(
+        body,
+        out_shape=outs,
+        in_specs=[vmem] * len(args),
+        out_specs=[vmem] * len(outs),
+        scratch_shapes=list(scratch),
+    )(*args)
+
+
+def pack_slots_kernel(cols, head_dim, query, key, value, out):
+    for col in range(cols):
+        half = col // 2
+        out[col, :, :head_dim] = query[:, col * head_dim : (col + 1) * head_dim]
+        for place, source in ((1, key), (2, value)):
+            out[col, :, place * head_dim : (place + 1) * head_dim] = source[
+                :, half * head_dim : (half + 1) * head_dim
+            ]
+
+
+def pack_wide_kernel(cols, gate, up, out):
+    part = gate.shape[1] // cols
+    for col in range(cols):
+        out[col, :, :part] = gate[:, col * part : (col + 1) * part]
+        out[col, :, part:] = up[:, col * part : (col + 1) * part]
+
+
+def open_wide_kernel(cols, wide, gate, up):
+    part = gate.shape[1] // cols
+    for col in range(cols):
+        gate[:, col * part : (col + 1) * part] = wide[col, :, :part].astype(jnp.float32)
+        up[:, col * part : (col + 1) * part] = wide[col, :, part:].astype(jnp.float32)
+
+
+def open_slots_kernel(cols, head_dim, slots, out):
+    for col in range(cols):
+        out[:, col * head_dim : (col + 1) * head_dim] = slots[col, :, :head_dim].astype(jnp.float32)
+    for half in range(cols // 2):
+        for place in (1, 2):
+            lanes = slice(place * head_dim, (place + 1) * head_dim)
+            begin = (cols + (place - 1) * (cols // 2) + half) * head_dim
+            out[:, begin : begin + head_dim] = slots[2 * half, :, lanes].astype(
+                jnp.float32
+            ) + slots[2 * half + 1, :, lanes].astype(jnp.float32)
 
 
 MESH = pl.DeviceIdType.MESH
@@ -359,10 +351,13 @@
     return call_kernel(body, [shaped] + list(swaps), outs, scratch, number)
 
 
-def last_sums(group_value, gains, number):
+def last_sums(group_value, widths, gains, number):
     sizes = [lax.axis_size(axis) for axis in ("dp", "row", "col")]
 
-    def body(value, gain, value_out, gain_out, value_in, landed, held, *sems):
+    def body(value, gain, *refs):
+        value_outs, gain_out = refs[: len(widths)], refs[len(widths)]
+        value_in, landed, held = refs[len(widths) + 1 : len(widths) + 4]
+        sems = refs[len(widths) + 4 :]
         value_sems, gain_sems = sems[:2], sems[2:]
         enter(("dp", "row", "col"))
         copies, groups = [], lax.axis_size("dp")
@@ -392,7 +387,6 @@
                 )
                 for step in range(1, size)
             ]
-            held[stage + 1] = held[stage]
             landed[stage, 0] = held[stage]
             for copy in sent:
                 copy.wait()
@@ -407,9 +401,13 @@
         total = value[...]
         for step in range(1, groups):
             total = total + value_in[step]
-        value_out[...] = total
-
-    outs = [jax.ShapeDtypeStruct(v.shape, jnp.float32) for v in (group_value, gains)]
+        begin = 0
+        for size, value_out in zip(widths, value_outs):
+            value_out[...] = total[:, begin : begin + size]
+            begin += size
+
+    outs = [jax.ShapeDtypeStruct((group_value.shape[0], size), jnp.float32) for size in widths]
+    outs.append(jax.ShapeDtypeStruct(gains.shape, jnp.float32))
     scratch = [
         pltpu.VMEM((sizes[0],) + group_value.shape, jnp.float32),
         pltpu.VMEM((3, max(sizes)) + gains.shape, jnp.float32),
@@ -457,18 +455,17 @@
     out_weight_full = lax.all_gather(out_weight, ("row", "col"), axis=0, tiled=True)
     out_full = lax.all_gather(out_grad, ("row", "col"), axis=0, tiled=True)
 
-    query_slots = query_weight.reshape(col_width, cols, head_dim)
-    key_slots = jnp.repeat(key_weight.reshape(col_width, cols // 2, head_dim), 2, axis=1)
-    value_slots = jnp.repeat(value_weight.reshape(col_width, cols // 2, head_dim), 2, axis=1)
-    slots = jnp.concatenate([query_slots, key_slots, value_slots], axis=2).transpose(1, 0, 2)
     hidden_width = gate_weight.shape[1] // cols
-    wide = jnp.concatenate(
-        [
-            gate_weight.reshape(col_width, cols, hidden_width),
-            up_weight.reshape(col_width, cols, hidden_width),
-        ],
-        axis=2,
-    ).transpose(1, 0, 2)
+    (slots,) = local_kernel(
+        functools.partial(pack_slots_kernel, cols, head_dim),
+        [query_weight, key_weight, value_weight],
+        [jax.ShapeDtypeStruct((cols, col_width, 3 * head_dim), jnp.bfloat16)],
+    )
+    (wide,) = local_kernel(
+        functools.partial(pack_wide_kernel, cols),
+        [gate_weight, up_weight],
+        [jax.ShapeDtypeStruct((cols, col_width, 2 * hidden_width), jnp.bfloat16)],
+    )
 
     input_blocks, slot_blocks = exchange([block_input], [slots], 0)
     input_full = input_blocks.reshape(length, width).astype(jnp.float32)
@@ -476,16 +473,29 @@
     first_full = head_norm(input_full, attn_norm)[0].astype(jnp.bfloat16)
     residual = block_input.astype(jnp.float32)
     scale_in = head_norm(residual, attn_norm)[1]
-    segment, position = segment_info(seq_lengths[0], length)
+    places = jnp.arange(length, dtype=jnp.int32)
+    position = segment_info(seq_lengths[0], length)[1]
+    begins = (places - position)[:, None]
     cosine, sine = rope_tables(position, head_dim)
+    cosine = jnp.concatenate([cosine, cosine], axis=1)
+    sine = jnp.concatenate([-sine, sine], axis=1)
     own_sums = dot(first_full, slot_weight)
-    query_raw = own_sums[:, :head_dim]
-    key_raw = own_sums[:, head_dim : 2 * head_dim]
-    value_raw = own_sums[:, 2 * head_dim :]
-    attn_low, log_total = head_forward(
-        query_raw, key_raw, value_raw, query_norm, key_norm, cosine, sine, segment
-    )
-    cat_blocks, wide_blocks = exchange([attn_low.T], [wide], 1)
+    longest = length // 2
+    head_gains = jnp.stack([query_norm, key_norm])
+    row_shape = jax.ShapeDtypeStruct((length, head_dim), jnp.bfloat16)
+    query_rot, key_rot, value_low, attn_low, attn_cols, log_total = local_kernel(
+        functools.partial(attend_kernel, longest),
+        [own_sums, head_gains, cosine, sine, begins],
+        [
+            row_shape,
+            row_shape,
+            row_shape,
+            row_shape,
+            jax.ShapeDtypeStruct((head_dim, length), jnp.bfloat16),
+            jax.ShapeDtypeStruct((length, 1), jnp.float32),
+        ],
+    )
+    cat_blocks, wide_blocks = exchange([attn_cols], [wide], 1)
     cat_full = cat_blocks.reshape(width, length)
     wide_weight = wide_blocks.reshape(width, 2 * hidden_width)
     middle = input_full + dot(cat_full, out_weight_full, 0, 0)
@@ -503,11 +513,8 @@
     up_low = (hidden_grad * activated).astype(jnp.bfloat16)
     wide_low = jnp.concatenate([gate_low, up_low], axis=1)
     (act_grad2,) = reduce_rows(dot(wide_low, wide_weight, 1, 1), [], 2)
-    down_sums = lax.psum_scatter(
-        dot(hidden, down_weight), ("row", "col"), scatter_dimension=0, tiled=True
-    )
+    down_part = dot(hidden, down_weight).astype(jnp.bfloat16)
     middle_own = own_rows(middle)
-    block_output = (middle_own + down_sums).astype(jnp.bfloat16)
     grad_down = dot(hidden, out_full, 0, 0)
     wide_grad = dot(second_full, wide_low, 0, 0).astype(jnp.bfloat16)
     middle_back, ffn_gain_grad = head_norm_back(
@@ -522,55 +529,59 @@
     middle_full = middle_blocks.reshape(length, width)
     grad_outweight = dot(attn_low, middle_full, 0, 0)
     cat_grad = dot(middle_full, out_weight, 1, 1).astype(jnp.bfloat16)
-    wide_grads = wide_grads.astype(jnp.float32).transpose(1, 0, 2)
-    grad_gate = wide_grads[:, :, :hidden_width].reshape(col_width, -1)
-    grad_up = wide_grads[:, :, hidden_width:].reshape(col_width, -1)
+    wide_shape = jax.ShapeDtypeStruct(gate_weight.shape, jnp.float32)
+    grad_gate, grad_up = local_kernel(
+        functools.partial(open_wide_kernel, cols), [wide_grads], [wide_shape, wide_shape]
+    )
+    down_part, cat_grad = lax.optimization_barrier((down_part, cat_grad))
+    down_sums = lax.psum_scatter(
+        down_part, ("row", "col"), scatter_dimension=0, tiled=True
+    ).astype(jnp.float32)
+    block_output = (middle_own + down_sums).astype(jnp.bfloat16)
+    accumulator = pltpu.VMEM((length, head_dim), jnp.float32)
+    own_slot, head_gain_grads = local_kernel(
+        functools.partial(attend_back_kernel, longest),
+        [query_rot, key_rot, value_low, attn_low, log_total, cat_grad]
+        + [own_sums, head_gains, cosine, sine, begins],
+        [
+            jax.ShapeDtypeStruct((length, 3 * head_dim), jnp.bfloat16),
+            jax.ShapeDtypeStruct((2, head_dim), jnp.float32),
+        ],
+        [accumulator] * 3,
+    )
+    own_slot, grad_outweight, grad_down = lax.optimization_barrier(
+        (own_slot, grad_outweight, grad_down)
+    )
     grad_outweight, grad_gate, grad_up, grad_down = lax.psum(
         (grad_outweight, grad_gate, grad_up, grad_down), "dp"
     )
-    query_low, key_low, value_low, query_gain, key_gain = head_backward(
-        query_raw,
-        key_raw,
-        value_raw,
-        query_norm,
-        key_norm,
-        cosine,
-        sine,
-        segment,
-        attn_low,
-        cat_grad,
-        log_total,
-    )
-    own_slot = jnp.concatenate([query_low, key_low, value_low], axis=1)
     slot_grad = dot(first_full, own_slot, 0, 0).astype(jnp.bfloat16)
     act_grad1, slot_grads = reduce_rows(
         dot(own_slot, slot_weight, 1, 1),
         [slot_grad.reshape(cols, col_width, 3 * head_dim)],
         4,
     )
-    slot_grads = slot_grads.astype(jnp.float32)
-    query_part = slot_grads[:, :, :head_dim].transpose(1, 0, 2).reshape(col_width, -1)
-    pairs = slot_grads.reshape(cols // 2, 2, col_width, 3 * head_dim).sum(axis=1).transpose(1, 0, 2)
-    key_part = pairs[:, :, head_dim : 2 * head_dim].reshape(col_width, -1)
-    value_part = pairs[:, :, 2 * head_dim :].reshape(col_width, -1)
+    widths = (cols * head_dim, cols // 2 * head_dim, cols // 2 * head_dim)
+    (slot_sums,) = local_kernel(
+        functools.partial(open_slots_kernel, cols, head_dim),
+        [slot_grads],
+        [jax.ShapeDtypeStruct((col_width, sum(widths)), jnp.float32)],
+    )
     input_back, attn_gain_grad = head_norm_back(act_grad1, residual, scale_in, attn_norm)
     input_grad = middle_grad + input_back
-    head_gains = jnp.concatenate(
-        [query_gain, key_gain, jnp.zeros((width - 2 * head_dim,), jnp.float32)]
-    )
-    gains = jnp.stack([attn_gain_grad, ffn_gain_grad, head_gains])
+    flat_gains = jnp.concatenate(
+        [head_gain_grads.reshape(-1), jnp.zeros((width - 2 * head_dim,), jnp.float32)]
+    )
+    gains = jnp.stack([attn_gain_grad, ffn_gain_grad, flat_gains])
     gains = jnp.concatenate([gains, jnp.zeros((5, width), jnp.float32)], axis=0)
-    group_sums, gain_sums = last_sums(
-        jnp.concatenate([query_part, key_part, value_part], axis=1), gains, 5
-    )
-    query_width, key_width = query_part.shape[1], key_part.shape[1]
+    grad_query, grad_key, grad_value, gain_sums = last_sums(slot_sums, widths, gains, 5)
     return (
         block_output,
         input_grad,
         gain_sums[0],
-        group_sums[:, :query_width],
-        group_sums[:, query_width : query_width + key_width],
-        group_sums[:, query_width + key_width :],
+        grad_query,
+        grad_key,
+        grad_value,
         gain_sums[2, :head_dim],
         gain_sums[2, head_dim : 2 * head_dim],
         grad_outweight,

time: 422 us -> 383 us (0.908)
  local copies, waits for them, and re-layouts: 69.4 us -> 19.3 us
  waiting for transfers between devices: 17.7 us -> 47 us
  matrix products: 56.1 us -> 36.1 us
  Pallas kernels: 229 us -> 248 us
  other arithmetic: 30.3 us -> 16.3 us
    pallas_call x0 -> x6, Pallas kernels: none -> 25.7 us  [local_kernel(): pl.pallas_call(body, out_shape=outs, in_specs=[vmem] * len(args), out_spe...]
    dot_general x14 -> x0, matrix products: 22 us -> none  [the longest x4 7.6 us: one_block(): jnp.dot(query_block, key_rows.T, preferred_element_type=jnp.float32)]
    all_gather x1, waiting for transfers between devices: 8.89 us -> 28.5 us  [shards(): out_full = lax.all_gather(out_grad, ('row', 'col'), axis=0, tiled=True)]
    psum x1, waiting for transfers between devices: 0.01 us -> 17.1 us  [shards(): lax.psum((grad_outweight, grad_gate, grad_up, grad_down), 'dp')]
    unnamed x94 -> x59, local copies, waits for them, and re-layouts: 24.9 us -> 12.5 us
    slice x9 -> x0, local copies, waits for them, and re-layouts: 12.4 us -> none  [the longest x2 5.11 us: shards(): grad_up = wide_grads[:, :, hidden_width:].reshape(col_width, -1)]
    dynamic_slice x16 -> x0, local copies, waits for them, and re-layouts: 7.84 us -> none  [the longest x4 3.75 us: attend(): lax.map(one_block, jnp.arange(length // block_rows, dtype=jnp.int32))]
    reduce_scatter x1, waiting for transfers between devices: 7.39 us -> 0.01 us  [shards(): lax.psum_scatter(down_part, ('row', 'col'), scatter_dimension=0, tiled=True)]
  transfers between devices with their start and end apart: 4 -> 4, of which waited for: 2 -> 2; matrix products, arithmetic and copies ran while one was open for 27% -> 10% of each run, Pallas kernels for 38% -> 47%
where the time goes in v2:
time: 383 us; the launch traced here: 382 us
  Pallas kernels  248 us (65%)
  waiting for transfers between devices  47 us (12%)
  matrix products  36.1 us (9%)
  local copies, waits for them, and re-layouts  19.3 us (5%)
  other arithmetic  16.3 us (4%)
  between operations  14.1 us (4%)
    pallas_call x6, Pallas kernels, call_kernel(): pl.pallas_call(body, out_shape=outs, in_specs=[vmem] * len(args), out_spe...  223 us
    dot_general x12, matrix products, dot(): lax.dot_general(left, right, (((left_dim,), (right_dim,)), ((), ())), pre...  36.1 us
    all_gather x1, waiting for transfers between devices, shards(): out_full = lax.all_gather(out_grad, ('row', 'col'), axis=0, tiled=True)  28.5 us
    pallas_call x6, Pallas kernels, local_kernel(): pl.pallas_call(body, out_shape=outs, in_specs=[vmem] * len(args), out_spe...  25.7 us
    psum x1, waiting for transfers between devices, shards(): lax.psum((grad_outweight, grad_gate, grad_up, grad_down), 'dp')  17.1 us
    unnamed x59, local copies, waits for them, and re-layouts  12.5 us
  transfers between devices with their start and end apart: 4, of which 2 were waited for; matrix products, arithmetic and copies ran while one was open for 10% of the time, Pallas kernels for 47%

profile of v2, /device:TPU:0, one launch (start us, length us, event | category | flops | bytes accessed | tf_op | source)
XLA Modules:
  0.0 381.6 jit_solution(12949287392751015119)
XLA Ops:
  7.2 0.7 all-gather.3.cloned.1.call-update
  8.0 0.7 all-gather.5.cloned.1.call-update
  8.7 0.0 reduce-scatter.2.cloned.1.call-start
  8.7 0.8 reduce-window.8
  9.6 0.7 select_reduce_fusion
  10.3 0.2 copy.45
  10.6 2.8 shard_map.240.refs_1_
  13.3 2.0 shard_map.237.refs_1_
  15.4 39.3 %shard_map.238 = (bf16[4,4,64,1024]{3,2,1,0:T(8,128)(2,1)}, bf16[4,256,192]{2,1,0:T(8,128)(2,1)}) custom-call(bf16[64,1024]{1,0:T(8,128)(2,1)} %refs_0_.1, bf16[4,256,192]{2,1,0:T(8,128)(2,1)} %shard_map.237.refs_1_), custom_call_target="tpu_custom_call" | custom-call | tf_op jit(solution)/shard_map/pallas_call | solution.py:220
  54.7 0.6 pad_maximum_fusion.5.gains.refs_7_
  55.3 1.9 fusion.15
  57.2 1.3 pad_maximum_fusion.3
  58.5 0.5 fusion
  59.0 0.9 subtract_subtract_fusion.begins.refs_10_
  59.9 0.5 fusion.2
  60.4 0.5 copy-done.14
  60.9 1.7 fusion.21.sums.refs_6_
  62.6 7.3 %shard_map.239 = (bf16[1024,64]{1,0:T(8,128)(2,1)}, bf16[1024,64]{1,0:T(8,128)(2,1)}, bf16[1024,64]{1,0:T(8,128)(2,1)}, bf16[1024,64]{1,0:T(8,128)(2,1)}, bf16[64,1024]{1,0:T(8,128)(2,1)}, /*index=5*/f32[1024,1]{1,0:T(8,128)}) custom-call(f32[1024,192]{1,0:T(8,128)} %fusion.21.sums.refs_6_, f32[2,64]{1,0:T(2,128)} %pad_maximum_fusion.5.gains.refs_7_, ...), custom_call_target="tpu_custom_call" | custom-call | tf_op jit(solution)/shard_map/pallas_call | solution.py:131
  70.0 45.6 %shard_map.241 = (bf16[4,4,64,1024]{3,2,1,0:T(8,128)(2,1)}, bf16[4,256,576]{2,1,0:T(8,128)(2,1)}) custom-call(bf16[64,1024]{1,0:T(8,128)(2,1)} %get-tuple-element.42.refs_0_, bf16[4,256,576]{2,1,0:T(8,128)(2,1)} %shard_map.240.refs_1_), custom_call_target="tpu_custom_call" | custom-call | tf_op jit(solution)/shard_map/pallas_call | solution.py:220
  115.7 5.1 %multiply_reduce_fusion = (f32[1024]{0:T(1024)S(1)}, f32[1024,1024]{1,0:T(8,128)S(1)}) fusion(bf16[1024,1024]{1,0:T(8,128)(2,1)} %bitcast.73, bf16[1024,1024]{1,0:T(8,128)(2,1)} %all-gather.3.cloned.1.call-done, bf16[4,4,64,1024]{3,2,1,0:T(8,128)(2,1)S(1)} %copy-done.1), kind=kOutput, calls=%fused_computation.10 | convolution fusion | flops 2151676928 | bytes 10489856 | tf_op jit(solution)/shard_map/dot_general | solution.py:421
  120.8 1.9 copy-done.2
  122.7 3.2 fusion.19
  126.0 28.5 %all-gather.5.cloned.1.call-done = bf16[1024,1024]{1,0:T(8,128)(2,1)} async-done(((bf16[64,1024]{1,0:T(8,128)(2,1)}), bf16[1024,1024]{1,0:T(8,128)(2,1)}) %all-gather.5.cloned.1.call-update) | async-done | bytes 2097168 | tf_op jit(solution)/shard_map/all_gather | solution.py:456
  154.5 4.4 %multiply_convert_fusion.2 = (bf16[1024,288]{0,1:T(8,128)(2,1)S(1)}, bf16[1024,288]{0,1:T(8,128)(2,1)S(1)}, bf16[1024,288]{0,1:T(8,128)(2,1)}) fusion(f32[1024,576]{0,1:T(8,128)} %fusion.19, bf16[1024,1024]{1,0:T(8,128)(2,1)} %all-gather.5.cloned.1.call-done, bf16[288,1024]{1,0:T(8,128)(2,1)S(1)} %copy-done), kind=kOutput, calls=%fused_computation.19 | convolution fusion | flops 608403456 | bytes 6815744 | tf_op jit(solution)/shard_map/dot_general | solution.py:421
  158.9 3.2 convolution_convert_fusion.2
  162.1 2.5 convolution_convert_fusion.3
  164.7 0.1 dynamic-slice.3
  164.7 28.6 %shard_map.242 = f32[64,1024]{1,0:T(8,128)} custom-call(bf16[4,4,64,1024]{3,2,1,0:T(8,128)(2,1)} %bitcast.57), custom_call_target="tpu_custom_call" | custom-call | tf_op jit(solution)/shard_map/pallas_call | solution.py:220
  193.4 1.3 multiply_reduce_fusion.1
  194.6 1.8 fusion.18.refs_0_
  196.5 2.5 copy.47
  198.9 39.5 %shard_map.243 = (bf16[4,4,64,1024]{3,2,1,0:T(8,128)(2,1)}, bf16[4,256,576]{2,1,0:T(8,128)(2,1)}) custom-call(bf16[64,1024]{1,0:T(8,128)(2,1)} %fusion.18.refs_0_, bf16[4,256,576]{2,1,0:T(8,128)(2,1)} %bitcast.54), custom_call_target="tpu_custom_call" | custom-call | tf_op jit(solution)/shard_map/pallas_call | solution.py:220
  238.5 3.0 convolution_convert_fusion.5.refs_5_
  241.5 2.7 convolution_convert_fusion.1
  244.2 0.3 all-reduce.4.cloned.1.call-start
  244.5 8.4 %shard_map.244 = (bf16[1024,192]{1,0:T(8,128)(2,1)}, f32[2,64]{1,0:T(2,128)}) custom-call(bf16[1024,64]{1,0:T(8,128)(2,1)} %get-tuple-element.47.refs_0_, bf16[1024,64]{1,0:T(8,128)(2,1)} %get-tuple-element.48.refs_1_, bf16[1024,64]{1,0:T(8,128)(2,1)} %get-tuple-element.49.refs_2_, bf16[1024,64]{1,0:T(8,128)(2,1)} %get-tuple-element.50.refs_3_, ...), custom_call_target="tpu_custom_call" | custom-call | tf_op jit(solution)/shard_map/pallas_call | solution.py:131
  252.9 3.0 fusion.22
  255.9 2.9 fusion.23
  258.8 3.0 shard_map.248
  261.8 0.1 rsqrt.36
  261.9 0.1 pad.4.clone
  262.0 0.7 copy-done.5
  262.7 0.1 fusion.14
  262.9 1.9 fusion.4
  264.8 0.1 reshape.187
  264.9 2.3 convolution_convert_fusion.4
  267.2 1.0 copy.50
  268.2 2.1 convolution_convert_fusion
  270.2 47.8 %shard_map.245 = (f32[64,1024]{1,0:T(8,128)}, bf16[4,256,192]{2,1,0:T(8,128)(2,1)}) custom-call(bf16[4,4,64,1024]{3,2,1,0:T(8,128)(2,1)} %bitcast.53, bf16[4,256,192]{2,1,0:T(8,128)(2,1)} %bitcast.55), custom_call_target="tpu_custom_call" | custom-call | tf_op jit(solution)/shard_map/pallas_call | solution.py:220
  318.0 2.1 shard_map.246.value
  320.1 1.2 fusion.13
  321.3 0.7 maximum_maximum_fusion.gain
  322.0 21.8 %shard_map.247 = (f32[256,256]{1,0:T(8,128)}, f32[256,128]{1,0:T(8,128)}, f32[256,128]{1,0:T(8,128)}, f32[8,1024]{1,0:T(8,128)}) custom-call(f32[256,512]{1,0:T(8,128)} %shard_map.246.value, f32[8,1024]{1,0:T(8,128)} %maximum_maximum_fusion.gain), custom_call_target="tpu_custom_call" | custom-call | tf_op jit(solution)/shard_map/pallas_call | solution.py:220
  343.9 1.3 slice_bitcast_fusion
  345.2 1.4 fusion.20
  346.7 2.1 fusion.12
  348.7 17.1 %all-reduce.4.cloned.1.call-done = (f32[64,1024]{1,0:T(8,128)}, f32[256,1152]{1,0:T(8,128)}, f32[256,1152]{1,0:T(8,128)}, f32[288,1024]{1,0:T(8,128)}) async-done(((f32[64,1024]{1,0:T(8,128)}, f32[256,1152]{1,0:T(8,128)}, f32[256,1152]{1,0:T(8,128)}, f32[288,1024]{1,0:T(8,128)}), (f32[64,1024]{1,0:T(8,128)}, f32[256,1152]{1,0:T(8,128)}, f32[256,1152]{1,0:T(8,128)}, ...) | async-done | bytes 3801104 | tf_op jit(solution)/shard_map/psum | solution.py:555
  365.8 1.8 copy.60
  367.6 0.7 copy.61
  368.3 0.7 copy.62
  368.9 1.7 copy.63
  370.6 2.5 copy.64
  373.0 1.0 copy.65
  374.1 1.0 copy.66
  (64 shorter events, 0.3 us)
Async XLA Ops:
  7.2 147.3 %copy-start = (bf16[288,1024]{1,0:T(8,128)(2,1)S(1)}, bf16[288,1024]{1,0:T(8,128)(2,1)}, u32[]{:S(2)}) copy-start(bf16[288,1024]{1,0:T(8,128)(2,1)} %param.27) | copy-start | bytes 1769476
  7.2 108.4 %all-gather.3.cloned.1.call-start = ((), (), s32[]{:S(2)}) async-start(), calls=%async_computation.1 | async-start | bytes 2228224 | tf_op jit(solution)/shard_map/all_gather | solution.py:455
  7.9 146.5 %all-gather.5.cloned.1.call-start = ((), (), s32[]{:S(2)}) async-start(), calls=%async_computation.2 | async-start | bytes 2228224 | tf_op jit(solution)/shard_map/all_gather | solution.py:456
  8.7 338.0 %reduce-scatter.2.cloned.1.call-start = ((), (), s32[]{:S(2)}) async-start(), calls=%async_computation.3 | async-start | bytes 2228224 | tf_op jit(solution)/shard_map/reduce_scatter | solution.py:537
  10.5 44.2 %copy-start.21 = (f32[64]{0:T(128)S(1)}, f32[64]{0:T(128)}, u32[]{:S(2)}) copy-start(f32[64]{0:T(128)} %param.22) | copy-start | bytes 772
  10.5 44.1 %copy-start.22 = (f32[64]{0:T(128)S(1)}, f32[64]{0:T(128)}, u32[]{:S(2)}) copy-start(f32[64]{0:T(128)} %param.21) | copy-start | bytes 772
  55.3 3.2 copy-start.1
  58.5 1.4 copy-start.20
  59.9 1.0 copy-start.14
  115.6 7.1 %copy-start.6 = (bf16[4,256,576]{2,1,0:T(8,128)(2,1)S(1)}, bf16[4,256,576]{2,1,0:T(8,128)(2,1)}, u32[]{:S(2)}) copy-start(bf16[4,256,576]{2,1,0:T(8,128)(2,1)} %get-tuple-element.44) | copy-start | bytes 3538948
  115.6 7.1 %copy-start.19 = (f32[1024]{0:T(1024)S(1)}, f32[1024]{0:T(1024)}, u32[]{:S(2)}) copy-start(f32[1024]{0:T(1024)} %param.24) | copy-start | bytes 12292
  120.8 2.0 copy-start.2
  154.5 4.4 %copy-start.7 = (bf16[4,256,576]{2,1,0:T(8,128)(2,1)S(1)}, bf16[4,256,576]{2,1,0:T(8,128)(2,1)}, u32[]{:S(2)}) copy-start(bf16[4,256,576]{2,1,0:T(8,128)(2,1)} %get-tuple-element.44) | copy-start | bytes 3538948
  158.9 3.3 copy-start.3
  164.6 30.0 %copy-start.10 = (bf16[64,1024]{1,0:T(8,128)(2,1)S(1)}, bf16[64,1024]{1,0:T(8,128)(2,1)}, u32[]{:S(2)}) copy-start(bf16[64,1024]{1,0:T(8,128)(2,1)} %param.16) | copy-start | bytes 393220
  196.5 42.0 %copy-start.13 = (bf16[64,1024]{1,0:T(8,128)(2,1)S(1)}, bf16[64,1024]{1,0:T(8,128)(2,1)}, u32[]{:S(2)}) copy-start(bf16[64,1024]{1,0:T(8,128)(2,1)} %param.23) | copy-start | bytes 393220
  238.4 3.1 copy-start.25
  244.2 121.6 %all-reduce.4.cloned.1.call-start = ((), (), s32[]{:S(2)}) async-start(), calls=%async_computation.4 | async-start | bytes 7602176 | tf_op jit(solution)/shard_map/psum | solution.py:555
  244.5 8.4 %copy-start.11 = (bf16[1024,64]{1,0:T(8,128)(2,1)S(1)}, bf16[1024,64]{1,0:T(8,128)(2,1)}, u32[]{:S(2)}) copy-start(bf16[1024,64]{1,0:T(8,128)(2,1)} %get-tuple-element.50.refs_3_) | copy-start | bytes 393220
  252.9 3.0 copy-start.23
  261.8 0.9 copy-start.5
  262.9 1.9 copy-start.24
  262.9 2.0 copy-start.16
  264.9 3.3 copy-start.15
  270.2 76.4 %copy-start.4 = (f32[64,1024]{1,0:T(8,128)S(1)}, f32[64,1024]{1,0:T(8,128)}, u32[]{:S(2)}) copy-start(f32[64,1024]{1,0:T(8,128)} %shard_map.242) | copy-start | bytes 786436
  318.0 28.6 %copy-start.12 = (f32[64,1024]{1,0:T(8,128)S(1)}, f32[64,1024]{1,0:T(8,128)}, u32[]{:S(2)}) copy-start(f32[64,1024]{1,0:T(8,128)} %get-tuple-element.55) | copy-start | bytes 786436
  343.9 23.8 %copy-start.18 = (f32[256,128]{1,0:T(8,128)S(1)}, f32[256,128]{1,0:T(8,128)}, u32[]{:S(2)}) copy-start(f32[256,128]{1,0:T(8,128)} %get-tuple-element.108) | copy-start | bytes 393220
  343.9 24.4 %copy-start.17 = (f32[256,128]{1,0:T(8,128)S(1)}, f32[256,128]{1,0:T(8,128)}, u32[]{:S(2)}) copy-start(f32[256,128]{1,0:T(8,128)} %get-tuple-element.109) | copy-start | bytes 393220
  365.8 7.2 %copy-start.9 = (f32[256,1152]{1,0:T(8,128)S(1)}, f32[256,1152]{1,0:T(8,128)}, u32[]{:S(2)}) copy-start(f32[256,1152]{1,0:T(8,128)} %get-tuple-element.115) | copy-start | bytes 3538948
  370.6 3.5 copy-start.8
Sparse Core Ops, SparseCore 0:
  10.8 77.2 all-gather.2
  90.9 63.4 all-gather.4
  244.3 95.5 reduce-scatter.1
  342.9 22.8 all-reduce.3

commit v3 on v2

--- a/solution.py
+++ b/solution.py
@@ -453,7 +453,6 @@
         return lax.dynamic_slice_in_dim(values, place, local_rows, 0)
 
     out_weight_full = lax.all_gather(out_weight, ("row", "col"), axis=0, tiled=True)
-    out_full = lax.all_gather(out_grad, ("row", "col"), axis=0, tiled=True)
 
     hidden_width = gate_weight.shape[1] // cols
     (slots,) = local_kernel(
@@ -495,7 +494,8 @@
             jax.ShapeDtypeStruct((length, 1), jnp.float32),
         ],
     )
-    cat_blocks, wide_blocks = exchange([attn_cols], [wide], 1)
+    cat_blocks, out_blocks, wide_blocks = exchange([attn_cols, out_grad], [wide], 1)
+    out_full = out_blocks.reshape(length, width)
     cat_full = cat_blocks.reshape(width, length)
     wide_weight = wide_blocks.reshape(width, 2 * hidden_width)
     middle = input_full + dot(cat_full, out_weight_full, 0, 0)
@@ -512,8 +512,12 @@
     )
     up_low = (hidden_grad * activated).astype(jnp.bfloat16)
     wide_low = jnp.concatenate([gate_low, up_low], axis=1)
-    (act_grad2,) = reduce_rows(dot(wide_low, wide_weight, 1, 1), [], 2)
-    down_part = dot(hidden, down_weight).astype(jnp.bfloat16)
+    both_parts = [
+        dot(wide_low, wide_weight, 1, 1).astype(jnp.bfloat16),
+        dot(hidden, down_weight).astype(jnp.bfloat16),
+    ]
+    (both_sums,) = reduce_rows(jnp.concatenate(both_parts, axis=1), [], 2)
+    act_grad2, down_sums = both_sums[:, :width], both_sums[:, width:]
     middle_own = own_rows(middle)
     grad_down = dot(hidden, out_full, 0, 0)
     wide_grad = dot(second_full, wide_low, 0, 0).astype(jnp.bfloat16)
@@ -533,10 +537,6 @@
     grad_gate, grad_up = local_kernel(
         functools.partial(open_wide_kernel, cols), [wide_grads], [wide_shape, wide_shape]
     )
-    down_part, cat_grad = lax.optimization_barrier((down_part, cat_grad))
-    down_sums = lax.psum_scatter(
-        down_part, ("row", "col"), scatter_dimension=0, tiled=True
-    ).astype(jnp.float32)
     block_output = (middle_own + down_sums).astype(jnp.bfloat16)
     accumulator = pltpu.VMEM((length, head_dim), jnp.float32)
     own_slot, head_gain_grads = local_kernel(
@@ -548,9 +548,6 @@
             jax.ShapeDtypeStruct((2, head_dim), jnp.float32),
         ],
         [accumulator] * 3,
-    )
-    own_slot, grad_outweight, grad_down = lax.optimization_barrier(
-        (own_slot, grad_outweight, grad_down)
     )
     grad_outweight, grad_gate, grad_up, grad_down = lax.psum(
         (grad_outweight, grad_gate, grad_up, grad_down), "dp"

time: 383 us -> 361 us (0.943)
  waiting for transfers between devices: 47 us -> 0.72 us
  Pallas kernels: 248 us -> 268 us
  local copies, waits for them, and re-layouts: 19.3 us -> 27.6 us
  matrix products: 36.1 us -> 28.3 us
  other arithmetic: 16.3 us -> 20.8 us
    all_gather x1 -> x0, waiting for transfers between devices: 28.5 us -> none  [shards(): out_full = lax.all_gather(out_grad, ('row', 'col'), axis=0, tiled=True)]
    pallas_call x6, Pallas kernels: 223 us -> 242 us  [call_kernel(): pl.pallas_call(body, out_shape=outs, in_specs=[vmem] * len(args), out_spe...]
    psum x1, waiting for transfers between devices: 17.1 us -> 0.01 us  [shards(): lax.psum((grad_outweight, grad_gate, grad_up, grad_down), 'dp')]
    dot_general x12, matrix products: 36.1 us -> 28.3 us  [dot(): lax.dot_general(left, right, (((left_dim,), (right_dim,)), ((), ())), pre...]
    concatenate x0 -> x1, local copies, waits for them, and re-layouts: none -> 6.5 us  [shards(): both_sums, = reduce_rows(jnp.concatenate(both_parts, axis=1), [], 2)]
    concatenate x0 -> x1, other arithmetic: none -> 4.65 us  [shards(): both_sums, = reduce_rows(jnp.concatenate(both_parts, axis=1), [], 2)]
    unnamed x59 -> x55, local copies, waits for them, and re-layouts: 12.5 us -> 11.8 us
  transfers between devices with their start and end apart: 4 -> 2, of which waited for: 2 -> 0; matrix products, arithmetic and copies ran while one was open for 10% -> 7% of each run, Pallas kernels for 47% -> 48%
where the time goes in v3:
time: 361 us; the launch traced here: 360 us
  Pallas kernels  268 us (74%)
  matrix products  28.3 us (8%)
  local copies, waits for them, and re-layouts  27.6 us (8%)
  other arithmetic  20.8 us (6%)
  between operations  14.4 us (4%)
    pallas_call x6, Pallas kernels, call_kernel(): pl.pallas_call(body, out_shape=outs, in_specs=[vmem] * len(args), out_spe...  242 us
    dot_general x12, matrix products, dot(): lax.dot_general(left, right, (((left_dim,), (right_dim,)), ((), ())), pre...  28.3 us
    pallas_call x6, Pallas kernels, local_kernel(): pl.pallas_call(body, out_shape=outs, in_specs=[vmem] * len(args), out_spe...  26.1 us
    unnamed x55, local copies, waits for them, and re-layouts  11.8 us
  transfers between devices with their start and end apart: 2, of which 0 were waited for; matrix products, arithmetic and copies ran while one was open for 7% of the time, Pallas kernels for 48%

profile of v3, /device:TPU:0, one launch (start us, length us, event | category | flops | bytes accessed | tf_op | source)
XLA Modules:
  0.0 360.2 jit_solution(1377605448921597032)
XLA Ops:
  7.2 0.0 all-gather.2.cloned.1.call-start
  7.2 0.7 all-gather.2.cloned.1.call-update
  7.9 0.0 all-reduce.4.cloned.1.call-start
  8.0 0.8 reduce-window.8
  8.8 0.7 select_reduce_fusion
  9.6 0.2 copy.48
  9.8 2.8 shard_map.240.refs_2_
  12.6 2.0 shard_map.237.refs_1_
  14.6 39.0 %shard_map.238 = (bf16[4,4,64,1024]{3,2,1,0:T(8,128)(2,1)}, bf16[4,256,192]{2,1,0:T(8,128)(2,1)}) custom-call(bf16[64,1024]{1,0:T(8,128)(2,1)} %refs_0_.1, bf16[4,256,192]{2,1,0:T(8,128)(2,1)} %shard_map.237.refs_1_), custom_call_target="tpu_custom_call" | custom-call | tf_op jit(solution)/shard_map/pallas_call | solution.py:220
  53.6 0.6 pad_maximum_fusion.6.gains.refs_7_
  54.2 1.9 fusion.15
  56.1 1.3 pad_maximum_fusion.4
  57.4 0.5 fusion
  57.9 0.8 subtract_subtract_fusion.begins.refs_10_
  58.8 0.5 fusion.2
  59.3 0.5 copy-done.15
  59.8 1.7 fusion.21.sums.refs_6_
  61.5 7.6 %shard_map.239 = (bf16[1024,64]{1,0:T(8,128)(2,1)}, bf16[1024,64]{1,0:T(8,128)(2,1)}, bf16[1024,64]{1,0:T(8,128)(2,1)}, bf16[1024,64]{1,0:T(8,128)(2,1)}, bf16[64,1024]{1,0:T(8,128)(2,1)}, /*index=5*/f32[1024,1]{1,0:T(8,128)}) custom-call(f32[1024,192]{1,0:T(8,128)} %fusion.21.sums.refs_6_, f32[2,64]{1,0:T(2,128)} %pad_maximum_fusion.6.gains.refs_7_, ...), custom_call_target="tpu_custom_call" | custom-call | tf_op jit(solution)/shard_map/pallas_call | solution.py:131
  69.1 62.3 %shard_map.241 = (bf16[4,4,64,1024]{3,2,1,0:T(8,128)(2,1)}, bf16[4,4,64,1024]{3,2,1,0:T(8,128)(2,1)}, bf16[4,256,576]{2,1,0:T(8,128)(2,1)}) custom-call(bf16[64,1024]{1,0:T(8,128)(2,1)} %get-tuple-element.38.refs_0_, bf16[64,1024]{1,0:T(8,128)(2,1)} %refs_1_.1, bf16[4,256,576]{2,1,0:T(8,128)(2,1)} %shard_map.240.refs_2_), custom_call_target="tpu_custom_call" | custom-call | tf_op jit(solution)/shard_map/pallas_call | solution.py:220
  131.5 5.1 %multiply_reduce_fusion = (f32[1024]{0:T(1024)S(1)}, f32[1024,1024]{1,0:T(8,128)S(1)}) fusion(bf16[1024,1024]{1,0:T(8,128)(2,1)} %bitcast.76, bf16[1024,1024]{1,0:T(8,128)(2,1)} %all-gather.2.cloned.1.call-done, bf16[4,4,64,1024]{3,2,1,0:T(8,128)(2,1)S(1)} %copy-done.2), kind=kOutput, calls=%fused_computation.11 | convolution fusion | flops 2151676928 | bytes 10489856 | tf_op jit(solution)/shard_map/dot_general | solution.py:421
  136.7 1.8 fusion.19
  138.5 1.2 copy-done.23
  139.7 1.3 multiply_convert_fusion.3
  141.0 3.1 convolution_convert_fusion.2
  144.2 2.5 convolution_convert_fusion.3
  146.7 1.8 fusion.23
  148.5 2.7 convolution_convert_fusion.1
  151.2 0.1 dynamic-slice.3
  151.3 2.4 copy.51
  153.7 4.6 %pad_maximum_fusion = bf16[1024,2048]{0,1:T(8,128)(2,1)} fusion(bf16[1024,1024]{0,1:T(8,128)(2,1)} %convolution_convert_fusion.1, bf16[1024,1024]{0,1:T(8,128)(2,1)} %convolution_convert_fusion.2), kind=kLoop, calls=%fused_computation | loop fusion | flops 8388608 | bytes 8388608 | tf_op jit(solution)/shard_map/concatenate | solution.py:519
  158.3 6.5 %copy.50 = bf16[1024,2048]{1,0:T(8,128)(2,1)} copy(bf16[1024,2048]{0,1:T(8,128)(2,1)} %pad_maximum_fusion) | data formatting | bytes 8388608 | tf_op jit(solution)/shard_map/concatenate | solution.py:519
  164.8 51.6 %shard_map.242 = f32[64,2048]{1,0:T(8,128)} custom-call(bf16[4,4,64,2048]{3,2,1,0:T(8,128)(2,1)} %bitcast.52), custom_call_target="tpu_custom_call" | custom-call | tf_op jit(solution)/shard_map/pallas_call | solution.py:220
  216.5 1.3 multiply_reduce_fusion.1
  217.8 1.8 fusion.18.refs_0_
  219.6 39.0 %shard_map.243 = (bf16[4,4,64,1024]{3,2,1,0:T(8,128)(2,1)}, bf16[4,256,576]{2,1,0:T(8,128)(2,1)}) custom-call(bf16[64,1024]{1,0:T(8,128)(2,1)} %fusion.18.refs_0_, bf16[4,256,576]{2,1,0:T(8,128)(2,1)} %bitcast.56), custom_call_target="tpu_custom_call" | custom-call | tf_op jit(solution)/shard_map/pallas_call | solution.py:220
  258.7 3.0 shard_map.248
  261.7 2.8 fusion.22
  264.5 0.1 rsqrt.36
  264.6 0.1 pad.4.clone
  264.7 0.7 copy-done.6
  265.4 0.1 fusion.14
  265.6 1.9 fusion.4
  267.5 0.8 convolution_convert_fusion.5
  268.2 0.9 copy.52.refs_5_
  269.1 8.5 %shard_map.244 = (bf16[1024,192]{1,0:T(8,128)(2,1)}, f32[2,64]{1,0:T(2,128)}) custom-call(bf16[1024,64]{1,0:T(8,128)(2,1)} %get-tuple-element.42.refs_0_, bf16[1024,64]{1,0:T(8,128)(2,1)} %get-tuple-element.43.refs_1_, bf16[1024,64]{1,0:T(8,128)(2,1)} %get-tuple-element.44.refs_2_, bf16[1024,64]{1,0:T(8,128)(2,1)} %get-tuple-element.45.refs_3_, ...), custom_call_target="tpu_custom_call" | custom-call | tf_op jit(solution)/shard_map/pallas_call | solution.py:131
  277.6 0.8 reshape.191
  278.4 2.5 convolution_convert_fusion.4
  280.9 2.0 copy.54
  282.9 2.1 convolution_convert_fusion
  285.1 35.9 %shard_map.245 = (f32[64,1024]{1,0:T(8,128)}, bf16[4,256,192]{2,1,0:T(8,128)(2,1)}) custom-call(bf16[4,4,64,1024]{3,2,1,0:T(8,128)(2,1)} %bitcast.55, bf16[4,256,192]{2,1,0:T(8,128)(2,1)} %bitcast.57), custom_call_target="tpu_custom_call" | custom-call | tf_op jit(solution)/shard_map/pallas_call | solution.py:220
  321.0 2.1 shard_map.246.value
  323.1 1.2 fusion.13
  324.3 0.7 maximum_maximum_fusion.gain
  325.0 14.4 %shard_map.247 = (f32[256,256]{1,0:T(8,128)}, f32[256,128]{1,0:T(8,128)}, f32[256,128]{1,0:T(8,128)}, f32[8,1024]{1,0:T(8,128)}) custom-call(f32[256,512]{1,0:T(8,128)} %shard_map.246.value, f32[8,1024]{1,0:T(8,128)} %maximum_maximum_fusion.gain), custom_call_target="tpu_custom_call" | custom-call | tf_op jit(solution)/shard_map/pallas_call | solution.py:220
  339.4 1.3 slice_bitcast_fusion
  340.7 1.4 fusion.20
  342.2 1.9 fusion.12
  344.1 1.8 copy.63
  345.8 0.7 copy.64
  346.5 0.7 copy.65
  347.1 1.7 copy.66
  348.8 2.5 copy.67
  351.3 1.0 copy.68
  352.3 1.0 copy.69
  (57 shorter events, 0.2 us)
Async XLA Ops:
  7.2 131.3 %copy-start = (bf16[288,1024]{1,0:T(8,128)(2,1)S(1)}, bf16[288,1024]{1,0:T(8,128)(2,1)}, u32[]{:S(2)}) copy-start(bf16[288,1024]{1,0:T(8,128)(2,1)} %param.27) | copy-start | bytes 1769476
  7.2 124.3 %all-gather.2.cloned.1.call-start = ((), (), s32[]{:S(2)}) async-start(), calls=%async_computation | async-start | bytes 2228224 | tf_op jit(solution)/shard_map/all_gather | solution.py:455
  7.9 336.1 %all-reduce.4.cloned.1.call-start = ((), (), s32[]{:S(2)}) async-start(), calls=%async_computation.1 | async-start | bytes 7602176 | tf_op jit(solution)/shard_map/psum | solution.py:552
  9.8 43.8 %copy-start.21 = (f32[64]{0:T(128)S(1)}, f32[64]{0:T(128)}, u32[]{:S(2)}) copy-start(f32[64]{0:T(128)} %param.22) | copy-start | bytes 772
  9.8 43.8 %copy-start.22 = (f32[64]{0:T(128)S(1)}, f32[64]{0:T(128)}, u32[]{:S(2)}) copy-start(f32[64]{0:T(128)} %param.21) | copy-start | bytes 772
  54.2 3.2 copy-start.2
  57.4 1.4 copy-start.20
  58.8 1.0 copy-start.15
  131.5 5.2 %copy-start.8 = (bf16[4,256,576]{2,1,0:T(8,128)(2,1)S(1)}, bf16[4,256,576]{2,1,0:T(8,128)(2,1)}, u32[]{:S(2)}) copy-start(bf16[4,256,576]{2,1,0:T(8,128)(2,1)} %get-tuple-element.41) | copy-start | bytes 3538948
  131.5 5.2 %copy-start.19 = (f32[1024]{0:T(1024)S(1)}, f32[1024]{0:T(1024)}, u32[]{:S(2)}) copy-start(f32[1024]{0:T(1024)} %param.24) | copy-start | bytes 12292
  136.6 7.5 %copy-start.4 = (f32[1024,1024]{1,0:T(8,128)}, f32[1024,1024]{1,0:T(8,128)S(1)}, u32[]{:S(2)}) copy-start(f32[1024,1024]{1,0:T(8,128)S(1)} %get-tuple-element.80) | copy-start | bytes 12582916
  136.7 3.1 copy-start.23
  164.8 53.0 %copy-start.9 = (bf16[64,1024]{1,0:T(8,128)(2,1)S(1)}, bf16[64,1024]{1,0:T(8,128)(2,1)}, u32[]{:S(2)}) copy-start(bf16[64,1024]{1,0:T(8,128)(2,1)} %refs_1_.1) | copy-start | bytes 393220
  216.5 45.2 %copy-start.12 = (bf16[1024,64]{1,0:T(8,128)(2,1)S(1)}, bf16[1024,64]{1,0:T(8,128)(2,1)}, u32[]{:S(2)}) copy-start(bf16[1024,64]{1,0:T(8,128)(2,1)} %get-tuple-element.45.refs_3_) | copy-start | bytes 393220
  264.5 0.9 copy-start.6
  265.6 1.9 copy-start.3
  265.6 1.9 copy-start.14
  269.1 9.3 %copy-start.7 = (bf16[1024,1024]{1,0:T(8,128)(2,1)S(1)}, bf16[1024,1024]{1,0:T(8,128)(2,1)}, u32[]{:S(2)}) copy-start(bf16[1024,1024]{1,0:T(8,128)(2,1)} %fusion.4) | copy-start | bytes 6291460
  278.4 4.5 %copy-start.16 = (bf16[1024,192]{1,0:T(8,128)(2,1)S(1)}, bf16[1024,192]{1,0:T(8,128)(2,1)}, u32[]{:S(2)}) copy-start(bf16[1024,192]{1,0:T(8,128)(2,1)} %get-tuple-element.48) | copy-start | bytes 1179652
  285.1 57.1 %copy-start.5 = (f32[64,2048]{1,0:T(8,128)S(1)}, f32[64,2048]{1,0:T(8,128)}, u32[]{:S(2)}) copy-start(f32[64,2048]{1,0:T(8,128)} %shard_map.242) | copy-start | bytes 1572868
  321.0 21.2 %copy-start.13 = (f32[64,1024]{1,0:T(8,128)S(1)}, f32[64,1024]{1,0:T(8,128)}, u32[]{:S(2)}) copy-start(f32[64,1024]{1,0:T(8,128)} %get-tuple-element.49) | copy-start | bytes 786436
  339.4 6.4 %copy-start.18 = (f32[256,128]{1,0:T(8,128)S(1)}, f32[256,128]{1,0:T(8,128)}, u32[]{:S(2)}) copy-start(f32[256,128]{1,0:T(8,128)} %get-tuple-element.100) | copy-start | bytes 393220
  339.4 7.1 %copy-start.17 = (f32[256,128]{1,0:T(8,128)S(1)}, f32[256,128]{1,0:T(8,128)}, u32[]{:S(2)}) copy-start(f32[256,128]{1,0:T(8,128)} %get-tuple-element.101) | copy-start | bytes 393220
  344.1 7.3 %copy-start.11 = (f32[256,1152]{1,0:T(8,128)S(1)}, f32[256,1152]{1,0:T(8,128)}, u32[]{:S(2)}) copy-start(f32[256,1152]{1,0:T(8,128)} %get-tuple-element.107) | copy-start | bytes 3538948
  348.8 3.5 copy-start.10
  348.8 4.5 %copy-start.1 = (bf16[288,1024]{1,0:T(8,128)(2,1)S(1)}, bf16[288,1024]{1,0:T(8,128)(2,1)}, u32[]{:S(2)}) copy-start(bf16[288,1024]{1,0:T(8,128)(2,1)} %param.27) | copy-start | bytes 1769476
Sparse Core Ops, SparseCore 0:
  10.8 78.2 all-gather.1
  264.7 29.3 all-reduce.3
